TPU v7x, 1024 devices: a whole 8x8x8 slice. The times are simulated.
1024 devices in a mesh: row: 32 (over y, z_lo, core), col: 32 (over z_hi, x).
Axes of the slice: x: 8, y: 8, z: 8 (z_hi: 4, z_lo: 2; z = z_hi * 2 + z_lo), core: 2. Of those that a mesh axis runs over, the one named last changes fastest.
Arguments:
- objects: float32 [2, 2, 8192, 8192], P(None, None, 'row', 'col'), may hold values from -5 to 5
- probe: float32 [2, 2, 128, 128], replicated, may hold values from -6 to 6
- amplitudes: bfloat16 [32, 32, 6, 128, 128], P('row', 'col'), may hold values from 0.29882812 to 3
- owners: int32 [32, 32, 6], P('row', 'col'), may hold values from 0 to 31, as said below
- off_rows: int32 [32, 32, 6], P('row', 'col'), may hold values from 0 to 256
- off_cols: int32 [32, 32, 6], P('row', 'col'), may hold values from 0 to 256
Outputs:
- gradient: float32 [2, 2, 8192, 8192], P(None, None, 'row', 'col')
Inputs may be any that keep to these rules, and one draw needn't show every extreme that they name: Each device's 6 positions go to owners of its own tile row whose tile column is the device's own plus one of -3, -2, -1, 1, 2, 3, 4, taken modulo 32; at most 2 of them to one owner, exactly 2 to one owner from some device of every tile row. Over all devices of a tile row, one owner receives exactly 12 positions and every other owner at most 7.
All inputs are finite; a program needn't handle non-finite values.
Results may differ from a plain program's by a relative error of at most 0.009.
Values may be sent and summed in bfloat16 or wider, within the bound.
A program may use at most 32 MiB of HBM per device.

v0:
```python
import math

import jax
import jax.numpy as jnp
from jax import lax
from jax.sharding import PartitionSpec as P

CAP = 2
RMAX = 12


FRESNEL = 24.0
REACH_OFFSETS = (-3, -2, -1, 1, 2, 3, 4)


def shifted(block, axis, distance):
    devices = range(lax.axis_size(axis))
    route = [((i - distance) % len(devices), i) for i in devices]
    return lax.ppermute(block, axis, route)


def padded(array, sides, width):
    for axis, dim in sides:
        size, length = (lax.axis_size(axis), array.shape[dim])
        up = [(i, (i + 1) % size) for i in range(size - 1)]
        down = [(j, i) for i, j in up]
        last = lax.slice_in_dim(array, length - width, length, axis=dim)
        first = lax.slice_in_dim(array, 0, width, axis=dim)
        before = lax.ppermute(last, axis, up)
        after = lax.ppermute(first, axis, down)
        array = jnp.concatenate([before, array, after], axis=dim)
    return array


def make_mats(width):
    idx = jnp.arange(width, dtype=jnp.int32)
    prod = idx[:, None] * idx[None, :] % width
    angle = prod.astype(jnp.float32) * (2.0 * math.pi / width)
    scale = 1.0 / math.sqrt(width)
    f_re = jnp.cos(angle) * scale
    f_im = -jnp.sin(angle) * scale
    centred = (idx + width // 2) % width - width // 2
    theta = (centred * centred).astype(jnp.float32) * (math.pi * FRESNEL / (width * width))
    d_re = jnp.cos(theta)
    d_im = -jnp.sin(theta)
    m_re = d_re[:, None] * f_re - d_im[:, None] * f_im
    m_im = d_re[:, None] * f_im + d_im[:, None] * f_re
    high = lax.Precision.HIGHEST
    k_re = jnp.dot(f_re, m_re, precision=high) + jnp.dot(f_im, m_im, precision=high)
    k_im = jnp.dot(f_re, m_im, precision=high) - jnp.dot(f_im, m_re, precision=high)
    f_re = f_re.astype(jnp.bfloat16)
    f_im = f_im.astype(jnp.bfloat16)
    k_re = k_re.astype(jnp.bfloat16)
    k_im = k_im.astype(jnp.bfloat16)

    def left_stack(a_re, a_im):
        return jnp.stack([jnp.stack([a_re, -a_im]), jnp.stack([a_im, a_re])])

    def right_stack(a_re, a_im):
        return jnp.stack([jnp.stack([a_re, a_im]), jnp.stack([-a_im, a_re])])

    return (
        left_stack(k_re, k_im),
        right_stack(k_re, k_im),
        left_stack(f_re, f_im),
        right_stack(f_re, f_im),
        left_stack(k_re, -k_im),
        right_stack(k_re, -k_im),
        left_stack(f_re, -f_im),
        right_stack(f_re, -f_im),
    )


def apply_left(table, field):
    return jnp.einsum("trpq,nrqs->ntps", table, field, preferred_element_type=jnp.float32)


def apply_right(field, table):
    return jnp.einsum("nrpq,rtqs->ntps", field, table, preferred_element_type=jnp.float32)


def cmul(first, second):
    a_re = first[..., 0, :, :]
    a_im = first[..., 1, :, :]
    b_re = second[..., 0, :, :]
    b_im = second[..., 1, :, :]
    return jnp.stack([a_re * b_re - a_im * b_im, a_re * b_im + a_im * b_re], axis=-3)


def conj(field):
    return jnp.stack([field[..., 0, :, :], -field[..., 1, :, :]], axis=-3)


def pattern_grad(window, probe, amp, valid, mats):
    k_left, k_right, f_left, f_right, kc_left, kc_right, fc_left, fc_right = mats
    psi_one = cmul(probe, window[0]).astype(jnp.bfloat16)
    upper = apply_left(k_left, psi_one).astype(jnp.bfloat16)
    phi = apply_right(upper, k_right)
    psi_two = cmul(phi, window[1]).astype(jnp.bfloat16)
    vfield = apply_left(f_left, psi_two).astype(jnp.bfloat16)
    far = apply_right(vfield, f_right)
    inten = jnp.sum(far * far, axis=(0, 1))
    ratio = amp.astype(jnp.float32) / jnp.maximum(jnp.sqrt(inten), 1.0)
    resid = (far * (valid * (1.0 - ratio))).astype(jnp.bfloat16)
    wfield = apply_left(fc_left, resid).astype(jnp.bfloat16)
    g_two = apply_right(wfield, fc_right)
    g_phi = cmul(conj(window[1]), g_two).astype(jnp.bfloat16)
    yfield = apply_left(kc_left, g_phi).astype(jnp.bfloat16)
    g_one = apply_right(yfield, kc_right)
    grad_one = jnp.sum(cmul(conj(probe), g_one), axis=0)
    grad_two = jnp.sum(cmul(conj(phi), g_two), axis=0)
    return jnp.stack([grad_one, grad_two])


def pad_axis(piece, axis, before, after):
    widths = [(0, 0)] * piece.ndim
    widths[axis] = (before, after)
    return jnp.pad(piece, widths)


def fold_bands(wide, border, rows, cols):
    top = wide[:, :, :border]
    middle = wide[:, :, 2 * border : 2 * border + rows]
    bottom = wide[:, :, rows + 3 * border :]
    folded = middle + pad_axis(top, 2, 0, rows - border) + pad_axis(bottom, 2, rows - border, 0)
    left = folded[:, :, :, :border]
    centre = folded[:, :, :, 2 * border : 2 * border + cols]
    right = folded[:, :, :, cols + 3 * border :]
    return centre + pad_axis(left, 3, 0, cols - border) + pad_axis(right, 3, cols - border, 0)


def local(objects, probe, amplitudes, owners, off_rows, off_cols):
    width = amplitudes.shape[-1]
    border = width // 2
    count = amplitudes.shape[2]
    kinds = len(REACH_OFFSETS)
    slots = CAP * kinds
    ncols = lax.axis_size("col")
    myself = lax.axis_index("col")
    rows = objects.shape[2]
    cols = objects.shape[3]
    mats = make_mats(width)
    dest = owners.reshape(count)
    rows_at = off_rows.reshape(count)
    cols_at = off_cols.reshape(count)
    apart = (dest - myself) % ncols
    kind_of = jnp.zeros_like(dest)
    for number, offset in enumerate(REACH_OFFSETS):
        kind_of = kind_of + number * (apart == offset % ncols).astype(jnp.int32)
    series = jnp.arange(count, dtype=jnp.int32)
    before = (dest[:, None] == dest[None, :]) & (series[None, :] < series[:, None])
    rank = jnp.sum(before.astype(jnp.int32), axis=1)
    target = kind_of * CAP + rank
    choose = jnp.arange(slots, dtype=jnp.int32)[:, None] == target[None, :]
    flat = amplitudes.reshape(count, width * width)
    sent = jnp.dot(choose.astype(jnp.bfloat16), flat, preferred_element_type=jnp.float32).astype(
        jnp.bfloat16
    )
    details = jnp.stack([rows_at, cols_at, jnp.ones_like(rows_at)], axis=1)
    sent_details = jnp.sum(choose.astype(jnp.int32)[:, :, None] * details[None, :, :], axis=1)
    got_amps = []
    got_details = []
    for number, offset in enumerate(REACH_OFFSETS):
        piece = sent[number * CAP : (number + 1) * CAP]
        piece_details = sent_details[number * CAP : (number + 1) * CAP]
        came, came_details = shifted((piece, piece_details), "col", offset)
        got_amps.append(came)
        got_details.append(came_details)
    arrived = jnp.concatenate(got_amps, axis=0)
    arrived_details = jnp.concatenate(got_details, axis=0)
    live = arrived_details[:, 2]
    place = jnp.cumsum(live) - live
    pick = (place[None, :] == jnp.arange(RMAX, dtype=jnp.int32)[:, None]) & (live[None, :] > 0)
    held = jnp.dot(pick.astype(jnp.bfloat16), arrived, preferred_element_type=jnp.float32)
    held = held.astype(jnp.bfloat16).reshape(RMAX, width, width)
    held_details = jnp.sum(pick.astype(jnp.int32)[:, :, None] * arrived_details[None, :, :], axis=1)
    extended = padded(objects, (("row", 2), ("col", 3)), border)

    def visit(carry, item):
        amp, detail = item
        zero = jnp.zeros((), jnp.int32)
        corner = (zero, zero, detail[0], detail[1])
        window = lax.dynamic_slice(extended, corner, (objects.shape[0], 2, width, width))
        valid = detail[2].astype(jnp.float32)
        grads = pattern_grad(window, probe, amp, valid, mats)
        current = lax.dynamic_slice(carry, corner, grads.shape)
        return (lax.dynamic_update_slice(carry, current + grads, corner), None)

    summed, _ = lax.scan(visit, jnp.zeros(extended.shape, jnp.float32), (held, held_details))
    wide = padded(summed, (("row", 2), ("col", 3)), border)
    result = fold_bands(wide, border, rows, cols)
    return result


def solution(mesh):
    placed = (
        P(None, None, "row", "col"),
        P(),
        P("row", "col", None, None, None),
        P("row", "col", None),
        P("row", "col", None),
        P("row", "col", None),
    )
    return jax.shard_map(
        local, mesh=mesh, in_specs=placed, out_specs=P(None, None, "row", "col"), check_vma=False
    )
```

profile of v0, /device:TPU:287, one launch (start us, length us, event | category | flops | bytes accessed | tf_op | source)
XLA Modules:
  0.0 497.7 jit_solution(18288173194276974907)
XLA Ops:
  3.2 11.4 %collective-permute-start.6 = (s32[2,3]{0,1:T(4,128)}, s32[2,3]{0,1:T(4,128)}, u32[]{:S(2)}, u32[]{:S(2)}) collective-permute-start(s32[2,3]{0,1:T(4,128)} %get-tuple-element.302), channel_id=1, source_target_pairs={{28,0},{29,1},{30,2},{31,3},{0,4},{1,5},{2,6},{3,7},{4,8},{5,9},{6... | collective-permute-start | bytes 80 | tf_op jit(solution)/shard_map/ppermute | solution.py:19
  14.7 4.4 collective-permute-start.5
  19.1 5.7 %collective-permute-start.4 = (s32[2,3]{0,1:T(4,128)}, s32[2,3]{0,1:T(4,128)}, u32[]{:S(2)}, u32[]{:S(2)}) collective-permute-start(s32[2,3]{0,1:T(4,128)} %get-tuple-element.304), channel_id=1, source_target_pairs={{30,0},{31,1},{0,2},{1,3},{2,4},{3,5},{4,6},{5,7},{6,8},{7,9},{8,1... | collective-permute-start | bytes 80 | tf_op jit(solution)/shard_map/ppermute | solution.py:19
  24.7 3.1 collective-permute-start.3
  27.9 2.2 collective-permute-start.2
  38.5 3.5 collective-permute-start
  42.0 8.8 %collective-permute-start.17 = (bf16[2,16384]{1,0:T(2,128)(2,1)}, bf16[2,16384]{1,0:T(2,128)(2,1)S(1)}, u32[]{:S(2)}, u32[]{:S(2)}) collective-permute-start(bf16[2,16384]{1,0:T(2,128)(2,1)} %get-tuple-element.283), channel_id=1, source_target_pairs={{28,0},{29,1},{30,2},{31,3},{0,4},{1,5},{2,6},{3,7},{4,8},{5,9},{6... | collective-permute-start | bytes 196616 | tf_op jit(solution)/shard_map/ppermute | solution.py:19
  50.7 3.2 collective-permute-start.16
  53.9 7.3 %collective-permute-start.15 = (bf16[2,16384]{1,0:T(2,128)(2,1)}, bf16[2,16384]{1,0:T(2,128)(2,1)}, u32[]{:S(2)}, u32[]{:S(2)}) collective-permute-start(bf16[2,16384]{1,0:T(2,128)(2,1)} %get-tuple-element.285), channel_id=1, source_target_pairs={{30,0},{31,1},{0,2},{1,3},{2,4},{3,5},{4,6},{5,7},{6,8},{7,9},{8,1... | collective-permute-start | bytes 196616 | tf_op jit(solution)/shard_map/ppermute | solution.py:19
  61.8 7.4 %collective-permute-start.7 = (f32[2,2,64,256]{2,3,1,0:T(8,128)}, f32[2,2,64,256]{2,3,1,0:T(8,128)S(1)}, u32[]{:S(2)}, u32[]{:S(2)}) collective-permute-start(f32[2,2,64,256]{2,3,1,0:T(8,128)} %get-tuple-element.281), channel_id=1, source_target_pairs={{0,32},{32,64},{64,96},{96,128},{128,160},{160,192},{192,224},{224... | collective-permute-start | bytes 786440 | tf_op jit(solution)/shard_map/ppermute | solution.py:29
  72.7 8.5 %collective-permute-done.7 = f32[2,2,64,256]{2,3,1,0:T(8,128)S(1)} collective-permute-done((f32[2,2,64,256]{2,3,1,0:T(8,128)}, f32[2,2,64,256]{2,3,1,0:T(8,128)S(1)}, u32[]{:S(2)}, u32[]{:S(2)}) %collective-permute-start.7) | collective-permute-done | bytes 262176 | tf_op jit(solution)/shard_map/ppermute | solution.py:29
  81.2 6.5 %collective-permute-start.14 = (bf16[2,16384]{1,0:T(2,128)(2,1)}, bf16[2,16384]{1,0:T(2,128)(2,1)}, u32[]{:S(2)}, u32[]{:S(2)}) collective-permute-start(bf16[2,16384]{1,0:T(2,128)(2,1)} %get-tuple-element.286), channel_id=1, source_target_pairs={{31,0},{0,1},{1,2},{2,3},{3,4},{4,5},{5,6},{6,7},{7,8},{8,9},{9,10... | collective-permute-start | bytes 196616 | tf_op jit(solution)/shard_map/ppermute | solution.py:19
  90.9 3.4 collective-permute-start.10
  100.4 20.3 %collective-permute-done.13 = bf16[2,16384]{1,0:T(2,128)(2,1)S(1)} collective-permute-done((bf16[2,16384]{1,0:T(2,128)(2,1)}, bf16[2,16384]{1,0:T(2,128)(2,1)S(1)}, u32[]{:S(2)}, u32[]{:S(2)}) %collective-permute-start.13) | collective-permute-done | bytes 65568 | tf_op jit(solution)/shard_map/ppermute | solution.py:19
  120.7 3.5 concatenate.21
  126.4 3.1 pad_maximum_fusion.1
  129.7 311.8 %while.12 = (s32[]{:T(128)}, f32[2,2,384,384]{2,3,1,0:T(8,128)S(1)}, s32[12,3]{1,0:T(8,128)S(1)}, f32[2,2,128,128]{2,3,1,0:T(8,128)S(1)}, f32[2,2,384,384]{2,3,1...) while((s32[]{:T(128)}, ...), condition=%wide.region_8.9_spmd, body=%wide.region_4.8_spmd.sunk | while | flops 271368192 | bytes 12681745 | solution.py:189
  153.1 3.4 dynamic_update_slice.6
  180.0 3.4 dynamic_update_slice.6
  206.9 3.1 dynamic_update_slice.6
  233.4 3.2 dynamic_update_slice.6
  260.1 3.1 dynamic_update_slice.6
  286.6 3.1 dynamic_update_slice.6
  378.2 2.0 multiply_reduce_fusion.4
  428.8 2.0 multiply_reduce_fusion.4
  441.5 2.0 copy.138
  446.6 2.4 collective-permute-start.19
  449.0 6.4 %collective-permute-done.18 = f32[2,2,64,384]{3,2,1,0:T(8,128)} collective-permute-done((f32[2,2,64,384]{3,2,1,0:T(8,128)S(1)}, f32[2,2,64,384]{3,2,1,0:T(8,128)}, u32[]{:S(2)}, u32[]{:S(2)}) %collective-permute-start.18) | collective-permute-done | bytes 393248 | tf_op jit(solution)/shard_map/ppermute | solution.py:29
  456.6 2.1 copy.141
  460.2 9.2 %collective-permute-start.20 = (f32[2,2,512,64]{2,3,1,0:T(8,128)S(1)}, f32[2,2,512,64]{2,3,1,0:T(8,128)S(1)}, u32[]{:S(2)}, u32[]{:S(2)}) collective-permute-start(f32[2,2,512,64]{2,3,1,0:T(8,128)S(1)} %get-tuple-element.275), channel_id=1, source_target_pairs={{0,1},{1,2},{2,3},{3,4},{4,5},{5,6},{6,7},{7,8},{8,9},{9,10},{10,1... | collective-permute-start | bytes 1572872 | tf_op jit(solution)/shard_map/ppermute | solution.py:29
  471.4 12.5 %collective-permute-done.20 = f32[2,2,512,64]{2,3,1,0:T(8,128)S(1)} collective-permute-done((f32[2,2,512,64]{2,3,1,0:T(8,128)S(1)}, f32[2,2,512,64]{2,3,1,0:T(8,128)S(1)}, u32[]{:S(2)}, u32[]{:S(2)}) %collective-permute-start.20) | collective-permute-done | bytes 524320 | tf_op jit(solution)/shard_map/ppermute | solution.py:29
  483.9 10.5 %collective-permute-done.21 = f32[2,2,512,64]{2,3,1,0:T(8,128)S(1)} collective-permute-done((f32[2,2,512,64]{2,3,1,0:T(8,128)S(1)}, f32[2,2,512,64]{2,3,1,0:T(8,128)S(1)}, u32[]{:S(2)}, u32[]{:S(2)}) %collective-permute-start.21) | collective-permute-done | bytes 524320 | tf_op jit(solution)/shard_map/ppermute | solution.py:30
  (501 shorter events, 270.2 us)
Async XLA Ops:
  0.0 32.8 %copy-start.10 = (f32[2,2,128,128]{3,2,1,0:T(8,128)S(1)}, f32[2,2,128,128]{3,2,1,0:T(8,128)}, u32[]{:S(2)}) copy-start(f32[2,2,128,128]{3,2,1,0:T(8,128)} %param.9) | copy-start | bytes 786436
  3.2 33.3 %collective-permute-start.6 = (s32[2,3]{0,1:T(4,128)}, s32[2,3]{0,1:T(4,128)}, u32[]{:S(2)}, u32[]{:S(2)}) collective-permute-start(s32[2,3]{0,1:T(4,128)} %get-tuple-element.302), channel_id=1, source_target_pairs={{28,0},{29,1},{30,2},{31,3},{0,4},{1,5},{2,6},{3,7},{4,8},{5,9},{6... | collective-permute-start | bytes 80 | tf_op jit(solution)/shard_map/ppermute | solution.py:19
  14.7 23.8 %collective-permute-start.5 = (s32[2,3]{0,1:T(4,128)}, s32[2,3]{0,1:T(4,128)}, u32[]{:S(2)}, u32[]{:S(2)}) collective-permute-start(s32[2,3]{0,1:T(4,128)} %get-tuple-element.303), channel_id=1, source_target_pairs={{29,0},{30,1},{31,2},{0,3},{1,4},{2,5},{3,6},{4,7},{5,8},{6,9},{7,... | collective-permute-start | bytes 80 | tf_op jit(solution)/shard_map/ppermute | solution.py:19
  19.1 22.9 %collective-permute-start.4 = (s32[2,3]{0,1:T(4,128)}, s32[2,3]{0,1:T(4,128)}, u32[]{:S(2)}, u32[]{:S(2)}) collective-permute-start(s32[2,3]{0,1:T(4,128)} %get-tuple-element.304), channel_id=1, source_target_pairs={{30,0},{31,1},{0,2},{1,3},{2,4},{3,5},{4,6},{5,7},{6,8},{7,9},{8,1... | collective-permute-start | bytes 80 | tf_op jit(solution)/shard_map/ppermute | solution.py:19
  24.7 26.0 %collective-permute-start.3 = (s32[2,3]{0,1:T(4,128)S(1)}, s32[2,3]{0,1:T(4,128)}, u32[]{:S(2)}, u32[]{:S(2)}) collective-permute-start(s32[2,3]{0,1:T(4,128)S(1)} %get-tuple-element.305), channel_id=1, source_target_pairs={{31,0},{0,1},{1,2},{2,3},{3,4},{4,5},{5,6},{6,7},{7,8},{8,9},{9,10... | collective-permute-start | bytes 80 | tf_op jit(solution)/shard_map/ppermute | solution.py:19
  27.9 26.1 %collective-permute-start.2 = (s32[2,3]{0,1:T(4,128)S(1)}, s32[2,3]{0,1:T(4,128)}, u32[]{:S(2)}, u32[]{:S(2)}) collective-permute-start(s32[2,3]{0,1:T(4,128)S(1)} %get-tuple-element.306), channel_id=1, source_target_pairs={{1,0},{2,1},{3,2},{4,3},{5,4},{6,5},{7,6},{8,7},{9,8},{10,9},{11,1... | collective-permute-start | bytes 80 | tf_op jit(solution)/shard_map/ppermute | solution.py:19
  36.5 24.7 %collective-permute-start.1 = (s32[2,3]{0,1:T(4,128)S(1)}, s32[2,3]{0,1:T(4,128)S(1)}, u32[]{:S(2)}, u32[]{:S(2)}) collective-permute-start(s32[2,3]{0,1:T(4,128)S(1)} %get-tuple-element.307), channel_id=1, source_target_pairs={{2,0},{3,1},{4,2},{5,3},{6,4},{7,5},{8,6},{9,7},{10,8},{11,9},{12,... | collective-permute-start | bytes 80 | tf_op jit(solution)/shard_map/ppermute | solution.py:19
  38.5 30.7 %collective-permute-start = (s32[2,3]{0,1:T(4,128)S(1)}, s32[2,3]{0,1:T(4,128)S(1)}, u32[]{:S(2)}, u32[]{:S(2)}) collective-permute-start(s32[2,3]{0,1:T(4,128)S(1)} %get-tuple-element.308), channel_id=1, source_target_pairs={{3,0},{4,1},{5,2},{6,3},{7,4},{8,5},{9,6},{10,7},{11,8},{12,9},{13... | collective-permute-start | bytes 80 | tf_op jit(solution)/shard_map/ppermute | solution.py:19
  42.0 49.0 %collective-permute-start.17 = (bf16[2,16384]{1,0:T(2,128)(2,1)}, bf16[2,16384]{1,0:T(2,128)(2,1)S(1)}, u32[]{:S(2)}, u32[]{:S(2)}) collective-permute-start(bf16[2,16384]{1,0:T(2,128)(2,1)} %get-tuple-element.283), channel_id=1, source_target_pairs={{28,0},{29,1},{30,2},{31,3},{0,4},{1,5},{2,6},{3,7},{4,8},{5,9},{6... | collective-permute-start | bytes 196616 | tf_op jit(solution)/shard_map/ppermute | solution.py:19
  50.7 43.6 %collective-permute-start.16 = (bf16[2,16384]{1,0:T(2,128)(2,1)}, bf16[2,16384]{1,0:T(2,128)(2,1)S(1)}, u32[]{:S(2)}, u32[]{:S(2)}) collective-permute-start(bf16[2,16384]{1,0:T(2,128)(2,1)} %get-tuple-element.284), channel_id=1, source_target_pairs={{29,0},{30,1},{31,2},{0,3},{1,4},{2,5},{3,6},{4,7},{5,8},{6,9},{7,... | collective-permute-start | bytes 196616 | tf_op jit(solution)/shard_map/ppermute | solution.py:19
  53.9 42.3 %collective-permute-start.15 = (bf16[2,16384]{1,0:T(2,128)(2,1)}, bf16[2,16384]{1,0:T(2,128)(2,1)}, u32[]{:S(2)}, u32[]{:S(2)}) collective-permute-start(bf16[2,16384]{1,0:T(2,128)(2,1)} %get-tuple-element.285), channel_id=1, source_target_pairs={{30,0},{31,1},{0,2},{1,3},{2,4},{3,5},{4,6},{5,7},{6,8},{7,9},{8,1... | collective-permute-start | bytes 196616 | tf_op jit(solution)/shard_map/ppermute | solution.py:19
  61.8 19.4 %collective-permute-start.7 = (f32[2,2,64,256]{2,3,1,0:T(8,128)}, f32[2,2,64,256]{2,3,1,0:T(8,128)S(1)}, u32[]{:S(2)}, u32[]{:S(2)}) collective-permute-start(f32[2,2,64,256]{2,3,1,0:T(8,128)} %get-tuple-element.281), channel_id=1, source_target_pairs={{0,32},{32,64},{64,96},{96,128},{128,160},{160,192},{192,224},{224... | collective-permute-start | bytes 786440 | tf_op jit(solution)/shard_map/ppermute | solution.py:29
  69.8 18.0 %collective-permute-start.8 = (f32[2,2,64,256]{2,3,1,0:T(8,128)S(1)}, f32[2,2,64,256]{2,3,1,0:T(8,128)S(1)}, u32[]{:S(2)}, u32[]{:S(2)}) collective-permute-start(f32[2,2,64,256]{2,3,1,0:T(8,128)S(1)} %get-tuple-element.282), channel_id=1, source_target_pairs={{32,0},{64,32},{96,64},{128,96},{160,128},{192,160},{224,192},{256... | collective-permute-start | bytes 786440 | tf_op jit(solution)/shard_map/ppermute | solution.py:30
  81.2 17.0 %collective-permute-start.14 = (bf16[2,16384]{1,0:T(2,128)(2,1)}, bf16[2,16384]{1,0:T(2,128)(2,1)}, u32[]{:S(2)}, u32[]{:S(2)}) collective-permute-start(bf16[2,16384]{1,0:T(2,128)(2,1)} %get-tuple-element.286), channel_id=1, source_target_pairs={{31,0},{0,1},{1,2},{2,3},{3,4},{4,5},{5,6},{6,7},{7,8},{8,9},{9,10... | collective-permute-start | bytes 196616 | tf_op jit(solution)/shard_map/ppermute | solution.py:19
  89.0 37.3 %collective-permute-start.9 = (f32[2,2,384,64]{2,3,1,0:T(8,128)}, f32[2,2,384,64]{2,3,1,0:T(8,128)}, u32[]{:S(2)}, u32[]{:S(2)}) collective-permute-start(f32[2,2,384,64]{2,3,1,0:T(8,128)} %get-tuple-element.279), channel_id=1, source_target_pairs={{0,1},{1,2},{2,3},{3,4},{4,5},{5,6},{6,7},{7,8},{8,9},{9,10},{10,1... | collective-permute-start | bytes 1179656 | tf_op jit(solution)/shard_map/ppermute | solution.py:29
  90.9 35.4 %collective-permute-start.10 = (f32[2,2,384,64]{2,3,1,0:T(8,128)}, f32[2,2,384,64]{2,3,1,0:T(8,128)}, u32[]{:S(2)}, u32[]{:S(2)}) collective-permute-start(f32[2,2,384,64]{2,3,1,0:T(8,128)} %get-tuple-element.280), channel_id=1, source_target_pairs={{1,0},{2,1},{3,2},{4,3},{5,4},{6,5},{7,6},{8,7},{9,8},{10,9},{11,1... | collective-permute-start | bytes 1179656 | tf_op jit(solution)/shard_map/ppermute | solution.py:30
  94.3 26.3 %collective-permute-start.13 = (bf16[2,16384]{1,0:T(2,128)(2,1)}, bf16[2,16384]{1,0:T(2,128)(2,1)S(1)}, u32[]{:S(2)}, u32[]{:S(2)}) collective-permute-start(bf16[2,16384]{1,0:T(2,128)(2,1)} %get-tuple-element.287), channel_id=1, source_target_pairs={{1,0},{2,1},{3,2},{4,3},{5,4},{6,5},{7,6},{8,7},{9,8},{10,9},{11,1... | collective-permute-start | bytes 196616 | tf_op jit(solution)/shard_map/ppermute | solution.py:19
  96.3 24.4 %collective-permute-start.12 = (bf16[2,16384]{1,0:T(2,128)(2,1)}, bf16[2,16384]{1,0:T(2,128)(2,1)S(1)}, u32[]{:S(2)}, u32[]{:S(2)}) collective-permute-start(bf16[2,16384]{1,0:T(2,128)(2,1)} %get-tuple-element.288), channel_id=1, source_target_pairs={{2,0},{3,1},{4,2},{5,3},{6,4},{7,5},{8,6},{9,7},{10,8},{11,9},{12,... | collective-permute-start | bytes 196616 | tf_op jit(solution)/shard_map/ppermute | solution.py:19
  98.2 22.4 %collective-permute-start.11 = (bf16[2,16384]{1,0:T(2,128)(2,1)}, bf16[2,16384]{1,0:T(2,128)(2,1)S(1)}, u32[]{:S(2)}, u32[]{:S(2)}) collective-permute-start(bf16[2,16384]{1,0:T(2,128)(2,1)} %get-tuple-element.289), channel_id=1, source_target_pairs={{3,0},{4,1},{5,2},{6,3},{7,4},{8,5},{9,6},{10,7},{11,8},{12,9},{13... | collective-permute-start | bytes 196616 | tf_op jit(solution)/shard_map/ppermute | solution.py:19
  156.6 14.6 %copy-start.2 = (bf16[2,2,128,128]{3,2,0,1:T(8,128)(2,1)}, bf16[2,2,128,128]{3,2,0,1:T(8,128)(2,1)S(1)}, u32[]{:S(2)}) copy-start(bf16[2,2,128,128]{3,2,0,1:T(8,128)(2,1)S(1)} %get-tuple-element.457) | copy-start | bytes 393220 | tf_op jit(solution)/shard_map/while
  236.7 14.6 %copy-start.2 = (bf16[2,2,128,128]{3,2,0,1:T(8,128)(2,1)}, bf16[2,2,128,128]{3,2,0,1:T(8,128)(2,1)S(1)}, u32[]{:S(2)}) copy-start(bf16[2,2,128,128]{3,2,0,1:T(8,128)(2,1)S(1)} %get-tuple-element.457) | copy-start | bytes 393220 | tf_op jit(solution)/shard_map/while
  315.0 14.6 %copy-start.2 = (bf16[2,2,128,128]{3,2,0,1:T(8,128)(2,1)}, bf16[2,2,128,128]{3,2,0,1:T(8,128)(2,1)S(1)}, u32[]{:S(2)}) copy-start(bf16[2,2,128,128]{3,2,0,1:T(8,128)(2,1)S(1)} %get-tuple-element.457) | copy-start | bytes 393220 | tf_op jit(solution)/shard_map/while
  340.3 14.6 %copy-start.2 = (bf16[2,2,128,128]{3,2,0,1:T(8,128)(2,1)}, bf16[2,2,128,128]{3,2,0,1:T(8,128)(2,1)S(1)}, u32[]{:S(2)}) copy-start(bf16[2,2,128,128]{3,2,0,1:T(8,128)(2,1)S(1)} %get-tuple-element.457) | copy-start | bytes 393220 | tf_op jit(solution)/shard_map/while
  365.6 14.6 %copy-start.2 = (bf16[2,2,128,128]{3,2,0,1:T(8,128)(2,1)}, bf16[2,2,128,128]{3,2,0,1:T(8,128)(2,1)S(1)}, u32[]{:S(2)}) copy-start(bf16[2,2,128,128]{3,2,0,1:T(8,128)(2,1)S(1)} %get-tuple-element.457) | copy-start | bytes 393220 | tf_op jit(solution)/shard_map/while
  390.9 14.6 %copy-start.2 = (bf16[2,2,128,128]{3,2,0,1:T(8,128)(2,1)}, bf16[2,2,128,128]{3,2,0,1:T(8,128)(2,1)S(1)}, u32[]{:S(2)}) copy-start(bf16[2,2,128,128]{3,2,0,1:T(8,128)(2,1)S(1)} %get-tuple-element.457) | copy-start | bytes 393220 | tf_op jit(solution)/shard_map/while
  416.2 14.6 %copy-start.2 = (bf16[2,2,128,128]{3,2,0,1:T(8,128)(2,1)}, bf16[2,2,128,128]{3,2,0,1:T(8,128)(2,1)S(1)}, u32[]{:S(2)}) copy-start(bf16[2,2,128,128]{3,2,0,1:T(8,128)(2,1)S(1)} %get-tuple-element.457) | copy-start | bytes 393220 | tf_op jit(solution)/shard_map/while
  444.6 10.7 %collective-permute-start.18 = (f32[2,2,64,384]{3,2,1,0:T(8,128)S(1)}, f32[2,2,64,384]{3,2,1,0:T(8,128)}, u32[]{:S(2)}, u32[]{:S(2)}) collective-permute-start(f32[2,2,64,384]{3,2,1,0:T(8,128)S(1)} %get-tuple-element.277), channel_id=1, source_target_pairs={{0,32},{32,64},{64,96},{96,128},{128,160},{160,192},{192,224},{224... | collective-permute-start | bytes 1179656 | tf_op jit(solution)/shard_map/ppermute | solution.py:29
  446.6 10.1 %collective-permute-start.19 = (f32[2,2,64,384]{3,2,1,0:T(8,128)S(1)}, f32[2,2,64,384]{3,2,1,0:T(8,128)}, u32[]{:S(2)}, u32[]{:S(2)}) collective-permute-start(f32[2,2,64,384]{3,2,1,0:T(8,128)S(1)} %get-tuple-element.278), channel_id=1, source_target_pairs={{32,0},{64,32},{96,64},{128,96},{160,128},{192,160},{224,192},{256... | collective-permute-start | bytes 1179656 | tf_op jit(solution)/shard_map/ppermute | solution.py:30
  458.8 35.7 %copy-start.7 = (f32[2,2,64,384]{2,3,1,0:T(8,128)S(1)}, f32[2,2,64,384]{2,3,1,0:T(8,128)}, u32[]{:S(2)}) copy-start(f32[2,2,64,384]{2,3,1,0:T(8,128)} %copy.141) | copy-start | bytes 1179652
  460.2 23.6 %collective-permute-start.20 = (f32[2,2,512,64]{2,3,1,0:T(8,128)S(1)}, f32[2,2,512,64]{2,3,1,0:T(8,128)S(1)}, u32[]{:S(2)}, u32[]{:S(2)}) collective-permute-start(f32[2,2,512,64]{2,3,1,0:T(8,128)S(1)} %get-tuple-element.275), channel_id=1, source_target_pairs={{0,1},{1,2},{2,3},{3,4},{4,5},{5,6},{6,7},{7,8},{8,9},{9,10},{10,1... | collective-permute-start | bytes 1572872 | tf_op jit(solution)/shard_map/ppermute | solution.py:29
  469.4 26.1 %copy-start.11 = (pred[256]{0:T(512)(128)(4,1)S(1)}, pred[256]{0:T(512)(128)(4,1)}, u32[]{:S(2)}) copy-start(pred[256]{0:T(512)(128)(4,1)} %constant.113.clone.1) | copy-start | bytes 772
  469.4 25.0 %collective-permute-start.21 = (f32[2,2,512,64]{2,3,1,0:T(8,128)S(1)}, f32[2,2,512,64]{2,3,1,0:T(8,128)S(1)}, u32[]{:S(2)}, u32[]{:S(2)}) collective-permute-start(f32[2,2,512,64]{2,3,1,0:T(8,128)S(1)} %get-tuple-element.276), channel_id=1, source_target_pairs={{1,0},{2,1},{3,2},{4,3},{5,4},{6,5},{7,6},{8,7},{9,8},{10,9},{11,1... | collective-permute-start | bytes 1572872 | tf_op jit(solution)/shard_map/ppermute | solution.py:30
  (81 other events, 704.2 us)
where the time goes:
time: 504 us; the launch traced here: 498 us
  other arithmetic  113 us (22%)
  local copies, waits for them, and re-layouts  98.9 us (20%)
  starting transfers between devices  93.6 us (19%)
  matrix products  77.3 us (15%)
  waiting for transfers between devices  58.3 us (12%)
  loops' own time  56.5 us (11%)
    dot_general x48, matrix products, apply_right(): jnp.einsum('nrpq,rtqs->ntps', field, table, preferred_element_type=jnp.fl...  73.5 us
    ppermute x14, starting transfers between devices, shifted(): return lax.ppermute(block, axis, route)  63.6 us
    another operation x1, loops' own time, local(): lax.scan(visit, jnp.zeros(extended.shape, jnp.float32), (held, held_detai...  56.5 us
    another operation x37, other arithmetic  46.5 us
    dynamic_update_slice x12, local copies, waits for them, and re-layouts, visit(): return (lax.dynamic_update_slice(carry, current + grads, corner), None)  30.3 us
    ppermute x4, waiting for transfers between devices, padded(): before = lax.ppermute(last, axis, up)  27.4 us
    ppermute x4, starting transfers between devices, padded(): before = lax.ppermute(last, axis, up)  20.4 us
    ppermute x14, waiting for transfers between devices, shifted(): return lax.ppermute(block, axis, route)  20.3 us
  transfers between devices with their start and end apart: 22, of which 5 were waited for; matrix products, arithmetic and copies ran while one was open for 3% of the time, Pallas kernels for 0%

commit v1 on v0

v1 whole, which is shorter than its diff:
```python
import functools
import math

import jax
import jax.numpy as jnp
import numpy as np
from jax import lax
from jax.experimental import pallas as pl
from jax.experimental.pallas import tpu as pltpu
from jax.sharding import PartitionSpec as P

MESH = pl.DeviceIdType.MESH
REACH = (-3, -2, -1, 1, 2, 3, 4)
KINDS = len(REACH)
CAP = 2
SLOTS = CAP * KINDS
RMAX = 12
FRESNEL = 24.0
F32 = jnp.float32
BF16 = jnp.bfloat16
N = 128
B = 64
T = 256
EXT = T + 2 * B
CH = 4
SIDES = ((-1, 0), (1, 0), (0, -1), (0, 1), (-1, -1), (-1, 1), (1, -1), (1, 1))
PARTNERS = SIDES + tuple((0, d) for d in (-4, -3, -2, 2, 3, 4))


def tables():
    k = np.arange(N)
    f = np.exp(-2j * np.pi * ((k[:, None] * k[None, :]) % N) / N) / math.sqrt(N)
    c = (k + N // 2) % N - N // 2
    d = np.exp(-1j * np.pi * FRESNEL * c * c / (N * N))
    kk = np.conj(f) @ (d[:, None] * f)

    def left(a):
        a = np.block([[a.real, -a.imag], [a.imag, a.real]]).astype(np.float32)
        return jnp.asarray(a).astype(BF16)

    return left(kk), left(np.conj(kk)), left(f), left(np.conj(f))


def at(side):
    nr, nc = lax.axis_size("row"), lax.axis_size("col")
    r, c = lax.axis_index("row"), lax.axis_index("col")
    return (lax.rem(r + side[0] + nr, nr), lax.rem(c + side[1] + nc, nc))


def greet(partners):
    barrier = pltpu.get_barrier_semaphore()
    for side in partners:
        pl.semaphore_signal(barrier, inc=1, device_id=at(side), device_id_type=MESH)
    pl.semaphore_wait(barrier, len(partners))


def exists(side):
    nr, nc = lax.axis_size("row"), lax.axis_size("col")
    r, c = lax.axis_index("row") + side[0], lax.axis_index("col") + side[1]
    inside = (r >= 0) & (r < nr) & (c >= 0) & (c < nc)
    return jnp.where(inside, 1.0, 0.0).astype(F32)


def send(src, dst, sems, n, side):
    copy = pltpu.make_async_remote_copy(
        src_ref=src, dst_ref=dst, send_sem=sems.at[0, n], recv_sem=sems.at[1, n],
        device_id=at(side), device_id_type=MESH,
    )
    copy.start()
    return copy


def lanes(rows):
    return lax.broadcasted_iota(jnp.int32, (rows, N), 1)


def pack(first, second, high):
    lane = lanes(first.shape[0])
    keep = (lane >= B) if high else (lane < B)
    return jnp.where(keep, first, pltpu.roll(second, B, 1)).astype(BF16)


def rows_of(dr):
    return {-1: (0, B), 0: (0, T), 1: (T - B, B)}[dr]


def side_buffers():
    return [pltpu.VMEM((2, 4, 2, B, N), BF16), pltpu.VMEM((2, 2, T, N), BF16), pltpu.VMEM((4, 2, B, N), BF16)]


def buffer_of(buffers, n):
    return buffers[0].at[n] if n < 2 else buffers[1].at[n - 2] if n < 4 else buffers[2].at[n - 4]


def gather_kernel(obj, amps, owners, offr, offc, ext, got_amps, got_meta, s0, s1, s2, r0, r1, r2, s_amp, s_meta, sems):
    nc = lax.axis_size("col")
    me = lax.axis_index("col")
    count = amps.shape[0]
    out, into = (s0, s1, s2), (r0, r1, r2)
    for n, (dr, dc) in enumerate(SIDES):
        start, size = rows_of(dr)
        if dc == 0:
            for q in range(4):
                for j in range(2):
                    s0[n, q, j] = obj[q, start:start + size, j * N:(j + 1) * N].astype(BF16)
        else:
            j = 0 if dc < 0 else 1
            for t in range(2):
                a = obj[2 * t, start:start + size, j * N:(j + 1) * N]
                b = obj[2 * t + 1, start:start + size, j * N:(j + 1) * N]
                if n < 4:
                    s1[n - 2, t] = pack(a, b, dc > 0)
                else:
                    s2[n - 4, t] = pack(a, b, dc > 0)
    dest = [owners[0, 0, j] for j in range(count)]
    apart = [lax.rem(d - me + nc, nc) for d in dest]
    rank = []
    for j in range(count):
        same = jnp.int32(0)
        for i in range(j):
            same = same + jnp.where(dest[i] == dest[j], 1, 0)
        rank.append(same)
    lane = lax.broadcasted_iota(jnp.int32, (8, N), 1)
    for k, offset in enumerate(REACH):
        meta = jnp.zeros((8, N), jnp.int32)
        for r in range(CAP):
            which, live, row, col = jnp.int32(0), jnp.int32(0), jnp.int32(0), jnp.int32(0)
            for j in range(count):
                hit = (apart[j] == offset % nc) & (rank[j] == r)
                which = jnp.where(hit, j, which)
                live = jnp.where(hit, 1, live)
                row = jnp.where(hit, offr[0, 0, j], row)
                col = jnp.where(hit, offc[0, 0, j], col)
            s_amp[k, r] = amps[which]
            for n, value in enumerate((live, row, col)):
                meta = jnp.where(lane == 4 * r + n, value, meta)
        s_meta[k] = meta
    greet(PARTNERS)
    copies = [send(buffer_of(out, n), buffer_of(into, n), sems, n, side) for n, side in enumerate(SIDES)]
    for k, offset in enumerate(REACH):
        copies.append(send(s_meta.at[k], got_meta.at[k], sems, 8 + k, (0, offset)))
    for k, offset in enumerate(REACH):
        copies.append(send(s_amp.at[k], got_amps.at[k], sems, 15 + k, (0, offset)))
    for q in range(4):
        for j in range(2):
            ext[q, 1 + j, B:B + T] = obj[q, :, j * N:(j + 1) * N]
    for n, (dr, dc) in enumerate(SIDES):
        copies[n].wait()
        there = exists((-dr, -dc))
        start, size = {-1: (B + T, B), 0: (B, T), 1: (0, B)}[dr]
        if dc == 0:
            for q in range(4):
                for j in range(2):
                    ext[q, 1 + j, start:start + size] = r0[n, q, j].astype(F32) * there
        else:
            j = 3 if dc < 0 else 0
            for t in range(2):
                x = (r1[n - 2, t] if n < 4 else r2[n - 4, t]).astype(F32) * there
                ext[2 * t, j, start:start + size] = x
                ext[2 * t + 1, j, start:start + size] = pltpu.roll(x, B, 1)
    for copy in copies[8:]:
        copy.wait()


def gather(obj, amps, owners, offr, offc):
    vmem, smem = pl.BlockSpec(memory_space=pltpu.VMEM), pl.BlockSpec(memory_space=pltpu.SMEM)
    return pl.pallas_call(
        gather_kernel,
        out_shape=(
            jax.ShapeDtypeStruct((4, CH, EXT, N), F32),
            jax.ShapeDtypeStruct((KINDS, CAP, N, N), BF16),
            jax.ShapeDtypeStruct((KINDS, 8, N), jnp.int32),
        ),
        in_specs=[vmem, vmem, smem, smem, smem],
        out_specs=(vmem, vmem, vmem),
        scratch_shapes=[
            *side_buffers(), *side_buffers(),
            pltpu.VMEM((KINDS, CAP, N, N), BF16),
            pltpu.VMEM((KINDS, 8, N), jnp.int32),
            pltpu.SemaphoreType.DMA((2, 22)),
        ],
        compiler_params=pltpu.CompilerParams(collective_id=0, has_side_effects=True, vmem_limit_bytes=32 << 20),
    )(obj, amps, owners, offr, offc)


def dot(a, b):
    return jnp.dot(a, b, preferred_element_type=F32)


def blocks(x):
    return x[:N, :N], x[:N, N:], x[N:, :N], x[N:, N:]


def quad(a, b, c, d):
    return jnp.concatenate([jnp.concatenate([a, b], axis=1), jnp.concatenate([c, d], axis=1)], axis=0)


def turned(x):
    a, b, c, d = blocks(x.astype(BF16))
    return quad(a, c, b, d)


def window(ext, q, row, base, shift):
    low = ext[q, base, pl.ds(row, N), :]
    high = ext[q, base + 1, pl.ds(row, N), :]
    return pltpu.roll(jnp.where(lanes(N) >= shift, low, high), N - shift, 1)


def forward(w, probe, kl, kr, fl, fr):
    psi = [(w[0] * probe[m, 0] - w[1] * probe[m, 1], w[0] * probe[m, 1] + w[1] * probe[m, 0]) for m in range(2)]
    x = quad(psi[0][0], psi[1][0], psi[0][1], psi[1][1]).astype(BF16)
    phi = dot(turned(dot(kl, x)), kr)
    a, b, c, d = blocks(phi)
    x = quad(a * w[2] - b * w[3], c * w[2] - d * w[3], a * w[3] + b * w[2], c * w[3] + d * w[2]).astype(BF16)
    return phi, dot(turned(dot(fl, x)), fr)


def backward(phi, far, amp, live, w2, probe, kl, kr, fl, fr):
    a, b, c, d = blocks(far)
    inten = (a * a + b * b) + (c * c + d * d)
    factor = live * (1.0 - amp * lax.rsqrt(jnp.maximum(inten, 1.0)))
    x = quad(a * factor, c * factor, b * factor, d * factor).astype(BF16)
    g2 = dot(turned(dot(fr, x)), fl)
    a, b, c, d = blocks(g2)
    wr, wi = w2
    x = quad(wr * a + wi * b, wr * c + wi * d, wr * b - wi * a, wr * d - wi * c).astype(BF16)
    pa, pb, pc, pd = blocks(phi)
    s2r = pa * a + pb * b + pc * c + pd * d
    s2i = pa * b - pb * a + pc * d - pd * c
    g1 = dot(turned(dot(kr, x)), kl)
    a, b, c, d = blocks(g1)
    s1r = probe[0, 0] * a + probe[0, 1] * b + probe[1, 0] * c + probe[1, 1] * d
    s1i = probe[0, 0] * b - probe[0, 1] * a + probe[1, 0] * d - probe[1, 1] * c
    return s1r, s1i, s2r, s2i


def positions_kernel(meta, ext, amps, probe, kl, kr, fl, fr, acc, order):
    acc[...] = jnp.zeros_like(acc)
    mats = (kl, kr, fl, fr)
    order[SLOTS] = 0
    count = jnp.int32(0)
    for i in range(SLOTS):
        order[count] = i
        count = count + meta[i // CAP, 0, 4 * (i % CAP)]
    order[count] = SLOTS

    def step(pair, carry):
        items = []
        for n in range(2):
            slot = order[2 * pair + n]
            live = jnp.where(slot < SLOTS, 1, 0)
            slot = jnp.minimum(slot, SLOTS - 1)
            kind, rank = slot // CAP, lax.rem(slot, CAP)
            row = meta[kind, 0, 4 * rank + 1] * live
            col = meta[kind, 0, 4 * rank + 2] * live + B
            base, shift = col // N, lax.rem(col, N)
            items.append((kind, rank, live.astype(F32), row, base, shift))
        ks = [m[...] for m in mats]
        ws = [[window(ext, q, row, base, shift) for q in range(4)] for _, _, _, row, base, shift in items]
        fw = [forward(w, probe, *ks) for w in ws]
        gs = [
            backward(*fw[n], amps[kind, rank].astype(F32), live, ws[n][2:], probe, *ks)
            for n, (kind, rank, live, _, _, _) in enumerate(items)
        ]
        for g, (_, _, _, row, base, shift) in zip(gs, items):
            for q in range(4):
                t = pltpu.roll(g[q], shift, 1)
                low = lanes(N) >= shift
                acc[q, base, pl.ds(row, N), :] += jnp.where(low, t, 0.0)
                acc[q, base + 1, pl.ds(row, N), :] += jnp.where(low, 0.0, t)
        return carry

    lax.fori_loop(0, (count + 1) // 2, step, 0)


def positions(meta, ext, amps, probe, mats):
    vmem, smem = pl.BlockSpec(memory_space=pltpu.VMEM), pl.BlockSpec(memory_space=pltpu.SMEM)
    return pl.pallas_call(
        positions_kernel,
        out_shape=jax.ShapeDtypeStruct((4, CH, EXT, N), F32),
        in_specs=[smem] + [vmem] * 7,
        out_specs=vmem,
        scratch_shapes=[pltpu.SMEM((SLOTS + 2,), jnp.int32)],
        compiler_params=pltpu.CompilerParams(vmem_limit_bytes=32 << 20),
    )(meta, ext, amps, probe, *mats)


def fold_kernel(acc, out, s0, s1, s2, r0, r1, r2, sems):
    send_to, into = (s0, s1, s2), (r0, r1, r2)
    for n, (dr, dc) in enumerate(SIDES):
        start, size = {-1: (0, B), 0: (B, T), 1: (B + T, B)}[dr]
        if dc == 0:
            for q in range(4):
                for j in range(2):
                    s0[n, q, j] = acc[q, 1 + j, start:start + size].astype(BF16)
        else:
            j = 0 if dc < 0 else 3
            for t in range(2):
                x = pack(acc[2 * t, j, start:start + size], acc[2 * t + 1, j, start:start + size], dc < 0)
                if n < 4:
                    s1[n - 2, t] = x
                else:
                    s2[n - 4, t] = x
    greet(SIDES)
    copies = [send(buffer_of(send_to, n), buffer_of(into, n), sems, n, side) for n, side in enumerate(SIDES)]
    for q in range(4):
        for j in range(2):
            out[q, :, j * N:(j + 1) * N] = acc[q, 1 + j, B:B + T]
    for n, (dr, dc) in enumerate(SIDES):
        copies[n].wait()
        there = exists((-dr, -dc))
        start, size = {-1: (T - B, B), 0: (0, T), 1: (0, B)}[dr]
        if dc == 0:
            for q in range(4):
                for j in range(2):
                    out[q, start:start + size, j * N:(j + 1) * N] += r0[n, q, j].astype(F32) * there
        else:
            j = 1 if dc < 0 else 0
            for t in range(2):
                x = (r1[n - 2, t] if n < 4 else r2[n - 4, t]).astype(F32) * there
                lane = lanes(size)
                mine = (lane >= B) if dc < 0 else (lane < B)
                out[2 * t, start:start + size, j * N:(j + 1) * N] += jnp.where(mine, x, 0.0)
                out[2 * t + 1, start:start + size, j * N:(j + 1) * N] += jnp.where(mine, pltpu.roll(x, B, 1), 0.0)


def fold(acc):
    vmem = pl.BlockSpec(memory_space=pltpu.VMEM)
    return pl.pallas_call(
        fold_kernel,
        out_shape=jax.ShapeDtypeStruct((4, T, T), F32),
        in_specs=[vmem],
        out_specs=vmem,
        scratch_shapes=[*side_buffers(), *side_buffers(), pltpu.SemaphoreType.DMA((2, 8))],
        compiler_params=pltpu.CompilerParams(collective_id=1, has_side_effects=True, vmem_limit_bytes=32 << 20),
    )(acc)


def local(objects, probe, amplitudes, owners, off_rows, off_cols):
    mats = tables()
    ext, amps, meta = gather(objects.reshape(4, T, T), amplitudes.reshape(-1, N, N), owners, off_rows, off_cols)
    acc = positions(meta, ext, amps, probe, mats)
    return fold(acc).reshape(objects.shape)


def solution(mesh):
    placed = (
        P(None, None, "row", "col"),
        P(),
        P("row", "col", None, None, None),
        P("row", "col", None),
        P("row", "col", None),
        P("row", "col", None),
    )
    return jax.shard_map(
        local, mesh=mesh, in_specs=placed, out_specs=P(None, None, "row", "col"), check_vma=False
    )
```

time: 504 us -> 83.5 us (0.17)
  the two profiles are of different devices: /device:TPU:287 before, /device:TPU:33 now
where the time goes in v1:
time: 83.5 us; the launch traced here: 83.2 us
  Pallas kernels  73.5 us (88%)
  local copies, waits for them, and re-layouts  9.65 us (12%)
    pallas_call x1, Pallas kernels, gather(): pl.pallas_call(gather_kernel, out_shape=(jax.ShapeDtypeStruct((4, CH, EXT...  44 us
    pallas_call x1, Pallas kernels, fold(): pl.pallas_call(fold_kernel, out_shape=jax.ShapeDtypeStruct((4, T, T), F32...  14.9 us
    pallas_call x1, Pallas kernels, positions(): pl.pallas_call(positions_kernel, out_shape=jax.ShapeDtypeStruct((4, CH, E...  14.6 us
    unnamed x21, local copies, waits for them, and re-layouts  9.65 us

profile of v1, /device:TPU:33, one launch (start us, length us, event | category | flops | bytes accessed | tf_op | source)
XLA Modules:
  0.0 83.2 jit_solution(5786297676010584978)
XLA Ops:
  0.0 0.0 copy-start
  0.0 1.2 %copy-done = f32[2,2,256,256]{3,2,1,0:T(8,128)S(1)} copy-done((f32[2,2,256,256]{3,2,1,0:T(8,128)S(1)}, f32[2,2,256,256]{3,2,1,0:T(8,128)}, u32[]{:S(2)}) %copy-start) | copy-done | bytes 1048600
  1.2 0.0 copy-start.2
  1.2 0.9 %copy-done.2 = bf16[1,1,6,128,128]{4,3,2,1,0:T(8,128)(2,1)S(1)} copy-done((bf16[1,1,6,128,128]{4,3,2,1,0:T(8,128)(2,1)S(1)}, bf16[1,1,6,128,128]{4,3,2,1,0:T(8,128)(2,1)}, u32[]{:S(2)}) %copy-start.2) | copy-done | bytes 196632
  2.2 0.0 copy-start.7
  2.2 0.7 copy-done.7
  2.8 0.0 copy-start.8
  2.8 0.7 copy-done.8
  3.5 0.0 copy-start.9
  3.5 0.7 copy-done.9
  4.1 44.0 %shard_map.100 = (f32[4,4,384,128]{3,2,1,0:T(8,128)S(1)}, bf16[7,2,128,128]{3,2,1,0:T(8,128)(2,1)S(1)}, s32[7,8,128]{2,1,0:T(8,128)S(1)}) custom-call(f32[4,256,256]{2,1,0:T(8,128)S(1)} %bitcast.4, bf16[6,128,128]{2,1,0:T(8,128)(2,1)S(1)} %bitcast.5, s32[1,1,6]{2,1,0:T(1,128)S(1)} %copy-done.7, s32[1,1,6]{2,1,0:T(1,128)S(1)} %copy-done.8, ...), custom_call_target="tpu_custom_call" | custom-call | tf_op jit(solution)/shard_map/pallas_call | solution.py:167
  48.2 0.0 copy-start.1
  48.2 0.9 %copy-done.1 = f32[2,2,128,128]{3,2,1,0:T(8,128)S(1)} copy-done((f32[2,2,128,128]{3,2,1,0:T(8,128)S(1)}, f32[2,2,128,128]{3,2,1,0:T(8,128)}, u32[]{:S(2)}) %copy-start.1) | copy-done | bytes 262168
  49.1 0.0 copy-start.3
  49.1 0.9 %copy-done.3 = bf16[256,256]{1,0:T(8,128)(2,1)S(1)} copy-done((bf16[256,256]{1,0:T(8,128)(2,1)S(1)}, bf16[256,256]{1,0:T(8,128)(2,1)}, u32[]{:S(2)}) %copy-start.3) | copy-done | bytes 131096
  50.0 0.0 copy-start.4
  50.0 0.9 %copy-done.4 = bf16[256,256]{1,0:T(8,128)(2,1)S(1)} copy-done((bf16[256,256]{1,0:T(8,128)(2,1)S(1)}, bf16[256,256]{1,0:T(8,128)(2,1)}, u32[]{:S(2)}) %copy-start.4) | copy-done | bytes 131096
  50.9 0.0 copy-start.5
  50.9 0.9 %copy-done.5 = bf16[256,256]{1,0:T(8,128)(2,1)S(1)} copy-done((bf16[256,256]{1,0:T(8,128)(2,1)S(1)}, bf16[256,256]{1,0:T(8,128)(2,1)}, u32[]{:S(2)}) %copy-start.5) | copy-done | bytes 131096
  51.8 0.0 copy-start.6
  51.8 0.9 %copy-done.6 = bf16[256,256]{1,0:T(8,128)(2,1)S(1)} copy-done((bf16[256,256]{1,0:T(8,128)(2,1)S(1)}, bf16[256,256]{1,0:T(8,128)(2,1)}, u32[]{:S(2)}) %copy-start.6) | copy-done | bytes 131096
  52.7 14.6 %shard_map.101.acc = f32[4,4,384,128]{3,2,1,0:T(8,128)S(1)} custom-call(s32[7,8,128]{2,1,0:T(8,128)S(1)} %get-tuple-element.8.meta, f32[4,4,384,128]{3,2,1,0:T(8,128)S(1)} %get-tuple-element.9.ext, bf16[7,2,128,128]{3,2,1,0:T(8,128)(2,1)S(1)} %get-tuple-element.10.amps, f32[2,2,128,128]{3,2,1,0:T(8,128)S(1)} %copy-done.1, bf16[256,256]{1,0:T(8,128)(2,1)S(1)} %copy-done.6, ...), custom_call_target="tpu_custom_call" | custom-call | tf_op jit(solution)/shard_map/pallas_call | solution.py:278
  67.3 14.9 %shard_map.102 = f32[4,256,256]{2,1,0:T(8,128)S(1)} custom-call(f32[4,4,384,128]{3,2,1,0:T(8,128)S(1)} %shard_map.101.acc), custom_call_target="tpu_custom_call" | custom-call | tf_op jit(solution)/shard_map/pallas_call | solution.py:329
  82.2 1.0 %copy.12 = f32[2,2,256,256]{3,2,1,0:T(8,128)} copy(f32[2,2,256,256]{3,2,1,0:T(8,128)S(1)} %bitcast.3) | data formatting | bytes 2097152
Async XLA Ops:
  0.0 1.2 %copy-start = (f32[2,2,256,256]{3,2,1,0:T(8,128)S(1)}, f32[2,2,256,256]{3,2,1,0:T(8,128)}, u32[]{:S(2)}) copy-start(f32[2,2,256,256]{3,2,1,0:T(8,128)} %param.10) | copy-start | bytes 3145732
  1.2 0.9 %copy-start.2 = (bf16[1,1,6,128,128]{4,3,2,1,0:T(8,128)(2,1)S(1)}, bf16[1,1,6,128,128]{4,3,2,1,0:T(8,128)(2,1)}, u32[]{:S(2)}) copy-start(bf16[1,1,6,128,128]{4,3,2,1,0:T(8,128)(2,1)} %param.12) | copy-start | bytes 589828
  2.2 0.7 copy-start.7
  2.8 0.7 copy-start.8
  3.5 0.7 copy-start.9
  48.2 1.0 %copy-start.1 = (f32[2,2,128,128]{3,2,1,0:T(8,128)S(1)}, f32[2,2,128,128]{3,2,1,0:T(8,128)}, u32[]{:S(2)}) copy-start(f32[2,2,128,128]{3,2,1,0:T(8,128)} %probe.1) | copy-start | bytes 786436
  49.1 0.9 %copy-start.3 = (bf16[256,256]{1,0:T(8,128)(2,1)S(1)}, bf16[256,256]{1,0:T(8,128)(2,1)}, u32[]{:S(2)}) copy-start(bf16[256,256]{1,0:T(8,128)(2,1)} %constant.19.fr) | copy-start | bytes 393220
  50.0 0.9 %copy-start.4 = (bf16[256,256]{1,0:T(8,128)(2,1)S(1)}, bf16[256,256]{1,0:T(8,128)(2,1)}, u32[]{:S(2)}) copy-start(bf16[256,256]{1,0:T(8,128)(2,1)} %constant.18.fl) | copy-start | bytes 393220
  50.9 0.9 %copy-start.5 = (bf16[256,256]{1,0:T(8,128)(2,1)S(1)}, bf16[256,256]{1,0:T(8,128)(2,1)}, u32[]{:S(2)}) copy-start(bf16[256,256]{1,0:T(8,128)(2,1)} %constant.17.kr) | copy-start | bytes 393220
  51.8 0.9 %copy-start.6 = (bf16[256,256]{1,0:T(8,128)(2,1)S(1)}, bf16[256,256]{1,0:T(8,128)(2,1)}, u32[]{:S(2)}) copy-start(bf16[256,256]{1,0:T(8,128)(2,1)} %constant.16.kl) | copy-start | bytes 393220

commit v2 on v0

v2 whole, which is shorter than its diff:
```python
import math

import jax
import jax.numpy as jnp
import numpy as np
from jax import lax
from jax.experimental import pallas as pl
from jax.experimental.pallas import tpu as pltpu
from jax.sharding import PartitionSpec as P

MESH = pl.DeviceIdType.MESH
REACH = (-3, -2, -1, 1, 2, 3, 4)
KINDS = len(REACH)
CAP = 2
SLOTS = CAP * KINDS
RMAX = 12
COUNT = 6
FRESNEL = 24.0
F32 = jnp.float32
BF16 = jnp.bfloat16
N = 128
B = 64
T = 256
EXT = T + 2 * B
CH = 4
SIDES = ((-1, 0), (1, 0), (0, -1), (0, 1), (-1, -1), (-1, 1), (1, -1), (1, 1))
PARTNERS = SIDES + tuple((0, d) for d in (-4, -3, -2, 2, 3, 4))
GROUP = 3


def tables():
    k = np.arange(N)
    f = np.exp(-2j * np.pi * ((k[:, None] * k[None, :]) % N) / N) / math.sqrt(N)
    c = (k + N // 2) % N - N // 2
    d = np.exp(-1j * np.pi * FRESNEL * c * c / (N * N))
    kk = np.conj(f) @ (d[:, None] * f)

    def left(a):
        return np.block([[a.real, -a.imag], [a.imag, a.real]]).astype(np.float32)

    return jnp.asarray(np.stack([left(kk), left(np.conj(kk)), left(f), left(np.conj(f))])).astype(BF16)


def at(side):
    nr, nc = lax.axis_size("row"), lax.axis_size("col")
    r, c = lax.axis_index("row"), lax.axis_index("col")
    return (lax.rem(r + side[0] + nr, nr), lax.rem(c + side[1] + nc, nc))


def exists(side):
    nr, nc = lax.axis_size("row"), lax.axis_size("col")
    r, c = lax.axis_index("row") + side[0], lax.axis_index("col") + side[1]
    inside = (r >= 0) & (r < nr) & (c >= 0) & (c < nc)
    return jnp.where(inside, 1.0, 0.0).astype(F32)


def lanes(rows):
    return lax.broadcasted_iota(jnp.int32, (rows, N), 1)


def pack(first, second, high):
    lane = lanes(first.shape[0])
    keep = (lane >= B) if high else (lane < B)
    return jnp.where(keep, first, pltpu.roll(second, B, 1)).astype(BF16)


def side_buffers():
    return [pltpu.VMEM((2, 2, 2, 2, B, N), BF16), pltpu.VMEM((2, 2, T, N), BF16), pltpu.VMEM((4, 2, B, N), BF16)]


def buffer_of(buffers, n, s):
    return buffers[0].at[n, s] if n < 2 else buffers[1].at[n - 2, s] if n < 4 else buffers[2].at[n - 4, s]


def dot(a, b):
    return jnp.dot(a, b, preferred_element_type=F32)


def blocks(x):
    return x[:N, :N], x[:N, N:], x[N:, :N], x[N:, N:]


def quad(a, b, c, d):
    return jnp.concatenate([jnp.concatenate([a, b], axis=1), jnp.concatenate([c, d], axis=1)], axis=0)


def both(left, x, right):
    a, b, c, d = blocks(dot(left, x).astype(BF16))
    return dot(quad(a, c, b, d), right)


def kernel(
    obj_h, amps_h, own_h, offr_h, offc_h, probe_h, mats_h, out_h,
    obj, amps, own, offr, offc, probe, mats, out,
    ext, s0, s1, s2, r0, r1, r2, f0, f1, f2, g0, g1, g2,
    s_amp, got_amp, s_meta, got_meta, meta, plan, masks, phi, far, win, gphi, tbuf, acc,
    sems, lsems,
):
    nc = lax.axis_size("col")
    me = lax.axis_index("col")
    used = [0]

    def send(src, dst, side):
        n = used[0]
        used[0] += 1
        copy = pltpu.make_async_remote_copy(
            src_ref=src, dst_ref=dst, send_sem=sems.at[0, n], recv_sem=sems.at[1, n],
            device_id=at(side), device_id_type=MESH,
        )
        copy.start()
        return copy

    barrier = pltpu.get_barrier_semaphore()
    for side in PARTNERS:
        pl.semaphore_signal(barrier, inc=1, device_id=at(side), device_id_type=MESH)

    def fetch(n, src, dst):
        copy = pltpu.make_async_copy(src, dst, lsems.at[n])
        copy.start()
        return copy

    in_ints = [fetch(n, a, b) for n, (a, b) in enumerate(((own_h, own), (offr_h, offr), (offc_h, offc)))]
    in_obj = [fetch(3 + s, obj_h.at[pl.ds(2 * s, 2)], obj.at[pl.ds(2 * s, 2)]) for s in range(2)]
    in_amps = fetch(5, amps_h, amps)
    in_probe, in_mats = fetch(6, probe_h, probe), fetch(7, mats_h, mats)

    for copy in in_ints:
        copy.wait()
    dest = [own[0, 0, j] for j in range(COUNT)]
    apart = [lax.rem(d - me + nc, nc) for d in dest]
    rank = []
    for j in range(COUNT):
        same = jnp.int32(0)
        for i in range(j):
            same = same + jnp.where(dest[i] == dest[j], 1, 0)
        rank.append(same)
    chosen = []
    lane8 = lanes(8)
    for k, offset in enumerate(REACH):
        line = jnp.zeros((8, N), jnp.int32)
        for r in range(CAP):
            which, live, row, col = jnp.int32(0), jnp.int32(0), jnp.int32(0), jnp.int32(0)
            for j in range(COUNT):
                hit = (apart[j] == offset % nc) & (rank[j] == r)
                which = jnp.where(hit, j, which)
                live = jnp.where(hit, 1, live)
                row = jnp.where(hit, offr[0, 0, j], row)
                col = jnp.where(hit, offc[0, 0, j], col)
            chosen.append(which)
            for n, value in enumerate((live, row, col)):
                line = jnp.where(lane8 == 4 * r + n, value, line)
        s_meta[k] = line

    def pack_object(s):
        for n, (dr, dc) in enumerate(SIDES):
            start, size = {-1: (0, B), 0: (0, T), 1: (T - B, B)}[dr]
            if dc == 0:
                for q in range(2):
                    for j in range(2):
                        s0[n, s, q, j] = obj[2 * s + q, start:start + size, j * N:(j + 1) * N].astype(BF16)
            else:
                j = 0 if dc < 0 else 1
                a = obj[2 * s, start:start + size, j * N:(j + 1) * N]
                b = obj[2 * s + 1, start:start + size, j * N:(j + 1) * N]
                if n < 4:
                    s1[n - 2, s] = pack(a, b, dc > 0)
                else:
                    s2[n - 4, s] = pack(a, b, dc > 0)

    in_obj[0].wait()
    pack_object(0)
    pl.semaphore_wait(barrier, len(PARTNERS))
    meta_copies = [send(s_meta.at[k], got_meta.at[k], (0, offset)) for k, offset in enumerate(REACH)]
    halo = [[send(buffer_of((s0, s1, s2), n, 0), buffer_of((r0, r1, r2), n, 0), side) for n, side in enumerate(SIDES)]]
    in_obj[1].wait()
    pack_object(1)
    halo.append([send(buffer_of((s0, s1, s2), n, 1), buffer_of((r0, r1, r2), n, 1), side) for n, side in enumerate(SIDES)])

    in_amps.wait()
    for k in range(KINDS):
        for r in range(CAP):
            s_amp[k, r] = amps[chosen[CAP * k + r]]
    for q in range(4):
        for j in range(2):
            ext[q, 1 + j, B:B + T] = obj[q, :, j * N:(j + 1) * N]

    def clear(n, carry):
        for q in range(4):
            tbuf[n, q, 0:T] = jnp.zeros((T, N), F32)
            tbuf[n, q, T + N:] = jnp.zeros((T, N), F32)
        return carry

    lax.fori_loop(0, RMAX, clear, 0)
    in_probe.wait()
    in_mats.wait()
    for copy in meta_copies:
        copy.wait()
    to_smem = fetch(8, got_meta, meta)
    to_smem.wait()

    lives = [meta[i // CAP, 0, 4 * (i % CAP)] for i in range(SLOTS)]
    places, total = [], jnp.int32(0)
    for live in lives:
        places.append(total)
        total = total + live
    for p in range(RMAX):
        slot, live = jnp.int32(0), jnp.int32(0)
        for i in range(SLOTS):
            hit = (places[i] == p) & (lives[i] == 1)
            slot = jnp.where(hit, i, slot)
            live = jnp.where(hit, 1, live)
        kind, rank_in = slot // CAP, lax.rem(slot, CAP)
        row = meta[kind, 0, 4 * rank_in + 1] * live
        col = meta[kind, 0, 4 * rank_in + 2] * live + B
        base, shift = col // N, lax.rem(col, N)
        for n, value in enumerate((kind, rank_in, live, row, base, shift)):
            plan[p, n] = value
        for k in range(CH):
            low = jnp.where(base == k, 1.0, 0.0).astype(F32)
            high = jnp.where(base + 1 == k, 1.0, 0.0).astype(F32)
            masks[p, k] = jnp.where(lane8 >= shift, low, high)

    def unpack_object(s):
        for n, (dr, dc) in enumerate(SIDES):
            halo[s][n].wait()
            there = exists((-dr, -dc))
            start, size = {-1: (B + T, B), 0: (B, T), 1: (0, B)}[dr]
            if dc == 0:
                for q in range(2):
                    for j in range(2):
                        ext[2 * s + q, 1 + j, start:start + size] = r0[n, s, q, j].astype(F32) * there
            else:
                j = 3 if dc < 0 else 0
                x = (r1[n - 2, s] if n < 4 else r2[n - 4, s]).astype(F32) * there
                ext[2 * s, j, start:start + size] = x
                ext[2 * s + 1, j, start:start + size] = pltpu.roll(x, B, 1)

    def window(q, p):
        row, base, shift = plan[p, 3], plan[p, 4], plan[p, 5]
        low = ext[q, base, pl.ds(row, N), :]
        high = ext[q, base + 1, pl.ds(row, N), :]
        return pltpu.roll(jnp.where(lanes(N) >= shift, low, high), N - shift, 1)

    def each(work):
        def step(n, carry):
            for i in range(GROUP):
                work(n * GROUP + i)
            return carry

        lax.fori_loop(0, RMAX // GROUP, step, 0)

    def first(p):
        wr, wi = window(0, p), window(1, p)
        psi = [(wr * probe[m, 0] - wi * probe[m, 1], wr * probe[m, 1] + wi * probe[m, 0]) for m in range(2)]
        x = quad(psi[0][0], psi[1][0], psi[0][1], psi[1][1]).astype(BF16)
        phi[p] = both(mats[0], x, mats[1])

    def second(p):
        wr, wi = window(2, p), window(3, p)
        win[p, 0], win[p, 1] = wr, wi
        a, b, c, d = blocks(phi[p])
        x = quad(a * wr - b * wi, c * wr - d * wi, a * wi + b * wr, c * wi + d * wr).astype(BF16)
        far[p] = both(mats[2], x, mats[3])

    def third(p):
        amp = got_amp[plan[p, 0], plan[p, 1]].astype(F32)
        live = plan[p, 2].astype(F32)
        a, b, c, d = blocks(far[p])
        inten = (a * a + b * b) + (c * c + d * d)
        factor = live * (1.0 - amp * lax.rsqrt(jnp.maximum(inten, 1.0)))
        x = quad(a * factor, c * factor, b * factor, d * factor).astype(BF16)
        a, b, c, d = blocks(both(mats[3], x, mats[2]))
        wr, wi = win[p, 0], win[p, 1]
        gphi[p] = quad(wr * a + wi * b, wr * c + wi * d, wr * b - wi * a, wr * d - wi * c).astype(BF16)
        pa, pb, pc, pd = blocks(phi[p])
        shift = plan[p, 5]
        tbuf[p, 2, T:T + N] = pltpu.roll(pa * a + pb * b + pc * c + pd * d, shift, 1)
        tbuf[p, 3, T:T + N] = pltpu.roll(pa * b - pb * a + pc * d - pd * c, shift, 1)

    def fourth(p):
        a, b, c, d = blocks(both(mats[1], gphi[p], mats[0]))
        shift = plan[p, 5]
        tbuf[p, 0, T:T + N] = pltpu.roll(probe[0, 0] * a + probe[0, 1] * b + probe[1, 0] * c + probe[1, 1] * d, shift, 1)
        tbuf[p, 1, T:T + N] = pltpu.roll(probe[0, 0] * b - probe[0, 1] * a + probe[1, 0] * d - probe[1, 1] * c, shift, 1)

    def scatter(s):
        def step(n, carry):
            q, start = 2 * s + n // (EXT // B), lax.rem(n, EXT // B) * B
            sums = [jnp.zeros((B // 8, 8, N), F32) for _ in range(CH)]
            for p in range(RMAX):
                t = tbuf[p, q, pl.ds(T - plan[p, 3] + start, B), :].reshape(B // 8, 8, N)
                for k in range(CH):
                    sums[k] = sums[k] + t * masks[p, k]
            for k in range(CH):
                acc[q, k, pl.ds(pl.multiple_of(start, B), B), :] = sums[k].reshape(B, N)
            return carry

        lax.fori_loop(0, 2 * (EXT // B), step, 0)

    def send_border(s):
        for n, (dr, dc) in enumerate(SIDES):
            start, size = {-1: (0, B), 0: (B, T), 1: (B + T, B)}[dr]
            if dc == 0:
                for q in range(2):
                    for j in range(2):
                        f0[n, s, q, j] = acc[2 * s + q, 1 + j, start:start + size].astype(BF16)
            else:
                j = 0 if dc < 0 else 3
                x = pack(acc[2 * s, j, start:start + size], acc[2 * s + 1, j, start:start + size], dc < 0)
                if n < 4:
                    f1[n - 2, s] = x
                else:
                    f2[n - 4, s] = x
        return [send(buffer_of((f0, f1, f2), n, s), buffer_of((g0, g1, g2), n, s), side) for n, side in enumerate(SIDES)]

    def add_border(s, copies):
        for q in range(2):
            for j in range(2):
                out[2 * s + q, :, j * N:(j + 1) * N] = acc[2 * s + q, 1 + j, B:B + T]
        for n, (dr, dc) in enumerate(SIDES):
            copies[n].wait()
            there = exists((-dr, -dc))
            start, size = {-1: (T - B, B), 0: (0, T), 1: (0, B)}[dr]
            if dc == 0:
                for q in range(2):
                    for j in range(2):
                        out[2 * s + q, start:start + size, j * N:(j + 1) * N] += g0[n, s, q, j].astype(F32) * there
            else:
                j = 1 if dc < 0 else 0
                x = (g1[n - 2, s] if n < 4 else g2[n - 4, s]).astype(F32) * there
                lane = lanes(size)
                mine = (lane >= B) if dc < 0 else (lane < B)
                out[2 * s, start:start + size, j * N:(j + 1) * N] += jnp.where(mine, x, 0.0)
                out[2 * s + 1, start:start + size, j * N:(j + 1) * N] += jnp.where(mine, pltpu.roll(x, B, 1), 0.0)

    unpack_object(0)
    amp_copies = [send(s_amp.at[k], got_amp.at[k], (0, offset)) for k, offset in enumerate(REACH)]
    each(first)
    unpack_object(1)
    each(second)
    for copy in amp_copies:
        copy.wait()
    each(third)
    scatter(1)
    late = send_border(1)
    each(fourth)
    scatter(0)
    last = send_border(0)
    add_border(1, late)
    back = [fetch(9, out.at[pl.ds(2, 2)], out_h.at[pl.ds(2, 2)])]
    add_border(0, last)
    back.append(fetch(10, out.at[pl.ds(0, 2)], out_h.at[pl.ds(0, 2)]))
    for copy in back:
        copy.wait()


def local(objects, probe, amplitudes, owners, off_rows, off_cols):
    anywhere = pl.BlockSpec(memory_space=pl.ANY)
    vmem, smem = pltpu.VMEM, pltpu.SMEM
    i32 = jnp.int32
    gradient = pl.pallas_call(
        kernel,
        out_shape=jax.ShapeDtypeStruct((4, T, T), F32),
        in_specs=[anywhere] * 7,
        out_specs=anywhere,
        scratch_shapes=[
            vmem((4, T, T), F32), vmem((COUNT, N, N), BF16), *[smem((1, 1, COUNT), i32)] * 3,
            vmem((2, 2, N, N), F32), vmem((4, 2 * N, 2 * N), BF16), vmem((4, T, T), F32),
            vmem((4, CH, EXT, N), F32), *side_buffers(), *side_buffers(), *side_buffers(), *side_buffers(),
            vmem((KINDS, CAP, N, N), BF16), vmem((KINDS, CAP, N, N), BF16),
            vmem((KINDS, 8, N), i32), vmem((KINDS, 8, N), i32), smem((KINDS, 8, N), i32), smem((RMAX, 8), i32),
            vmem((RMAX, CH, 8, N), F32), vmem((RMAX, 2 * N, 2 * N), F32), vmem((RMAX, 2 * N, 2 * N), F32),
            vmem((RMAX, 2, N, N), F32), vmem((RMAX, 2 * N, 2 * N), BF16),
            vmem((RMAX, 4, 2 * T + N, N), F32), vmem((4, CH, EXT, N), F32),
            pltpu.SemaphoreType.DMA((2, 2 * KINDS + 4 * len(SIDES))), pltpu.SemaphoreType.DMA((11,)),
        ],
        compiler_params=pltpu.CompilerParams(collective_id=0, has_side_effects=True, vmem_limit_bytes=56 << 20),
    )(objects.reshape(4, T, T), amplitudes.reshape(COUNT, N, N), owners, off_rows, off_cols, probe, tables())
    return gradient.reshape(objects.shape)


def solution(mesh):
    placed = (
        P(None, None, "row", "col"),
        P(),
        P("row", "col", None, None, None),
        P("row", "col", None),
        P("row", "col", None),
        P("row", "col", None),
    )
    return jax.shard_map(
        local, mesh=mesh, in_specs=placed, out_specs=P(None, None, "row", "col"), check_vma=False
    )
```

time: 504 us -> 67.6 us (0.13)
  the two profiles are of different devices: /device:TPU:287 before, /device:TPU:1 now
where the time goes in v2:
time: 67.6 us; the launch traced here: 66.8 us
  Pallas kernels  64.5 us (95%)
  local copies, waits for them, and re-layouts  2.29 us (3%)
    pallas_call x1, Pallas kernels, local(): pl.pallas_call(kernel, out_shape=jax.ShapeDtypeStruct((4, T, T), F32), in...  64.5 us
    unnamed x1, local copies, waits for them, and re-layouts  2.29 us

profile of v2, /device:TPU:1, one launch (start us, length us, event | category | flops | bytes accessed | tf_op | source)
XLA Modules:
  0.0 66.8 jit_solution(4163147697856185385)
XLA Ops:
  0.0 64.5 %shard_map.73 = f32[4,256,256]{2,1,0:T(8,128)} custom-call(f32[4,256,256]{2,1,0:T(8,128)} %bitcast.4, bf16[6,128,128]{2,1,0:T(8,128)(2,1)} %bitcast.5, s32[1,1,6]{2,1,0:T(1,128)} %own_h.1, s32[1,1,6]{2,1,0:T(1,128)} %offr_h.1, s32[1,1,6]{2,1,0:T(1,128)} %offc_h.1, f32[2,2,128,128]{3,2,1,0:T(8,128)} %probe_h.1, bf16[4,256,256]{2,1,0:T(8,128)(2,1)} %constant.7.mats_h), custom_call_target="tpu_custom_call" | custom-call | tf_op jit(solution)/shard_map/pallas_call | solution.py:361
  64.6 2.3 %copy.9 = f32[2,2,256,256]{3,2,1,0:T(8,128)} copy(f32[2,2,256,256]{3,2,1,0:T(8,128)} %bitcast.3) | data formatting | bytes 2097152

commit v3 on v2

--- a/solution.py
+++ b/solution.py
@@ -24,8 +24,10 @@
 EXT = T + 2 * B
 CH = 4
 SIDES = ((-1, 0), (1, 0), (0, -1), (0, 1), (-1, -1), (-1, 1), (1, -1), (1, 1))
-PARTNERS = SIDES + tuple((0, d) for d in (-4, -3, -2, 2, 3, 4))
-GROUP = 3
+XS = 8
+PARTNERS = SIDES + tuple((0, d) for d in (-4, -3, -2, 2, 3, 4, -XS, XS))
+THIRDS = 3
+GROUP = 6
 
 
 def tables():
@@ -93,20 +95,23 @@
     obj_h, amps_h, own_h, offr_h, offc_h, probe_h, mats_h, out_h,
     obj, amps, own, offr, offc, probe, mats, out,
     ext, s0, s1, s2, r0, r1, r2, f0, f1, f2, g0, g1, g2,
-    s_amp, got_amp, s_meta, got_meta, meta, plan, masks, phi, far, win, gphi, tbuf, acc,
+    s_amp, got_amp, passing, s_meta, got_meta, meta, plan, masks, phi, far, win, gphi, rows, parts, acc,
     sems, lsems,
 ):
     nc = lax.axis_size("col")
     me = lax.axis_index("col")
     used = [0]
 
-    def send(src, dst, side):
+    def prepare(src, dst, side, arrival=None):
         n = used[0]
         used[0] += 1
-        copy = pltpu.make_async_remote_copy(
-            src_ref=src, dst_ref=dst, send_sem=sems.at[0, n], recv_sem=sems.at[1, n],
+        return pltpu.make_async_remote_copy(
+            src_ref=src, dst_ref=dst, send_sem=sems.at[0, n], recv_sem=sems.at[1, n if arrival is None else arrival],
             device_id=at(side), device_id_type=MESH,
         )
+
+    def send(src, dst, side):
+        copy = prepare(src, dst, side)
         copy.start()
         return copy
 
@@ -123,6 +128,30 @@
     in_obj = [fetch(3 + s, obj_h.at[pl.ds(2 * s, 2)], obj.at[pl.ds(2 * s, 2)]) for s in range(2)]
     in_amps = fetch(5, amps_h, amps)
     in_probe, in_mats = fetch(6, probe_h, probe), fetch(7, mats_h, mats)
+
+    def pack_object(s):
+        for n, (dr, dc) in enumerate(SIDES):
+            start, size = {-1: (0, B), 0: (0, T), 1: (T - B, B)}[dr]
+            if dc == 0:
+                for q in range(2):
+                    for j in range(2):
+                        s0[n, s, q, j] = obj[2 * s + q, start:start + size, j * N:(j + 1) * N].astype(BF16)
+            else:
+                j = 0 if dc < 0 else 1
+                a = obj[2 * s, start:start + size, j * N:(j + 1) * N]
+                b = obj[2 * s + 1, start:start + size, j * N:(j + 1) * N]
+                if n < 4:
+                    s1[n - 2, s] = pack(a, b, dc > 0)
+                else:
+                    s2[n - 4, s] = pack(a, b, dc > 0)
+
+    in_obj[0].wait()
+    pack_object(0)
+    pl.semaphore_wait(barrier, len(PARTNERS))
+    halo = [[send(buffer_of((s0, s1, s2), n, 0), buffer_of((r0, r1, r2), n, 0), side) for n, side in enumerate(SIDES)]]
+    in_obj[1].wait()
+    pack_object(1)
+    halo.append([send(buffer_of((s0, s1, s2), n, 1), buffer_of((r0, r1, r2), n, 1), side) for n, side in enumerate(SIDES)])
 
     for copy in in_ints:
         copy.wait()
@@ -151,46 +180,58 @@
                 line = jnp.where(lane8 == 4 * r + n, value, line)
         s_meta[k] = line
 
-    def pack_object(s):
-        for n, (dr, dc) in enumerate(SIDES):
-            start, size = {-1: (0, B), 0: (0, T), 1: (T - B, B)}[dr]
-            if dc == 0:
-                for q in range(2):
-                    for j in range(2):
-                        s0[n, s, q, j] = obj[2 * s + q, start:start + size, j * N:(j + 1) * N].astype(BF16)
-            else:
-                j = 0 if dc < 0 else 1
-                a = obj[2 * s, start:start + size, j * N:(j + 1) * N]
-                b = obj[2 * s + 1, start:start + size, j * N:(j + 1) * N]
-                if n < 4:
-                    s1[n - 2, s] = pack(a, b, dc > 0)
-                else:
-                    s2[n - 4, s] = pack(a, b, dc > 0)
-
-    in_obj[0].wait()
-    pack_object(0)
-    pl.semaphore_wait(barrier, len(PARTNERS))
     meta_copies = [send(s_meta.at[k], got_meta.at[k], (0, offset)) for k, offset in enumerate(REACH)]
-    halo = [[send(buffer_of((s0, s1, s2), n, 0), buffer_of((r0, r1, r2), n, 0), side) for n, side in enumerate(SIDES)]]
-    in_obj[1].wait()
-    pack_object(1)
-    halo.append([send(buffer_of((s0, s1, s2), n, 1), buffer_of((r0, r1, r2), n, 1), side) for n, side in enumerate(SIDES)])
-
     in_amps.wait()
     for k in range(KINDS):
         for r in range(CAP):
             s_amp[k, r] = amps[chosen[CAP * k + r]]
+
+    x = lax.rem(me, XS)
+    straight, detour, onward, turns = [], [], [], []
+    for k, offset in enumerate(REACH):
+        step = XS if offset > 0 else -XS
+        turns.append(x == (XS - offset if offset > 0 else -1 - offset))
+        arrival = used[0]
+        straight.append(prepare(s_amp.at[k], got_amp.at[k], (0, offset)))
+        detour.append(prepare(s_amp.at[k], passing, (0, step)))
+        onward.append(prepare(passing, got_amp.at[k], (0, offset - step), arrival))
+
+    def start_amps():
+        for k in range(KINDS):
+            @pl.when(turns[k])
+            def _():
+                detour[k].start()
+
+            @pl.when(jnp.logical_not(turns[k]))
+            def _():
+                straight[k].start()
+
+    def pass_on():
+        for k in range(KINDS):
+            @pl.when(turns[k])
+            def _():
+                detour[k].wait_recv()
+                onward[k].start()
+
+    def end_amps():
+        for k in range(KINDS):
+            straight[k].wait_recv()
+
+            @pl.when(turns[k])
+            def _():
+                detour[k].wait_send()
+                onward[k].wait_send()
+
+            @pl.when(jnp.logical_not(turns[k]))
+            def _():
+                straight[k].wait_send()
+
+    start_amps()
+
     for q in range(4):
         for j in range(2):
             ext[q, 1 + j, B:B + T] = obj[q, :, j * N:(j + 1) * N]
 
-    def clear(n, carry):
-        for q in range(4):
-            tbuf[n, q, 0:T] = jnp.zeros((T, N), F32)
-            tbuf[n, q, T + N:] = jnp.zeros((T, N), F32)
-        return carry
-
-    lax.fori_loop(0, RMAX, clear, 0)
     in_probe.wait()
     in_mats.wait()
     for copy in meta_copies:
@@ -215,10 +256,12 @@
         base, shift = col // N, lax.rem(col, N)
         for n, value in enumerate((kind, rank_in, live, row, base, shift)):
             plan[p, n] = value
-        for k in range(CH):
+        for k in range(THIRDS):
             low = jnp.where(base == k, 1.0, 0.0).astype(F32)
-            high = jnp.where(base + 1 == k, 1.0, 0.0).astype(F32)
+            high = jnp.where((base + 1 == k) | (base + 1 == k + THIRDS), 1.0, 0.0).astype(F32)
             masks[p, k] = jnp.where(lane8 >= shift, low, high)
+        away = lax.broadcasted_iota(jnp.int32, (EXT, N), 0) - lanes(EXT)
+        rows[:, p * N:(p + 1) * N] = jnp.where(away == row, 1.0, 0.0).astype(BF16)
 
     def unpack_object(s):
         for n, (dr, dc) in enumerate(SIDES):
@@ -262,6 +305,13 @@
         x = quad(a * wr - b * wi, c * wr - d * wi, a * wi + b * wr, c * wi + d * wr).astype(BF16)
         far[p] = both(mats[2], x, mats[3])
 
+    def place(p, q, grad):
+        t = pltpu.roll(grad, plan[p, 5], 1).reshape(N // 8, 8, N)
+        for k in range(THIRDS):
+            at_k = (t * masks[p, k]).reshape(N, N).astype(BF16)
+            start = pl.multiple_of(p * N, N)
+            parts[pl.ds(start, N), (THIRDS * q + k) * N:(THIRDS * q + k + 1) * N] = at_k
+
     def third(p):
         amp = got_amp[plan[p, 0], plan[p, 1]].astype(F32)
         live = plan[p, 2].astype(F32)
@@ -273,29 +323,21 @@
         wr, wi = win[p, 0], win[p, 1]
         gphi[p] = quad(wr * a + wi * b, wr * c + wi * d, wr * b - wi * a, wr * d - wi * c).astype(BF16)
         pa, pb, pc, pd = blocks(phi[p])
-        shift = plan[p, 5]
-        tbuf[p, 2, T:T + N] = pltpu.roll(pa * a + pb * b + pc * c + pd * d, shift, 1)
-        tbuf[p, 3, T:T + N] = pltpu.roll(pa * b - pb * a + pc * d - pd * c, shift, 1)
+        place(p, 0, pa * a + pb * b + pc * c + pd * d)
+        place(p, 1, pa * b - pb * a + pc * d - pd * c)
 
     def fourth(p):
         a, b, c, d = blocks(both(mats[1], gphi[p], mats[0]))
-        shift = plan[p, 5]
-        tbuf[p, 0, T:T + N] = pltpu.roll(probe[0, 0] * a + probe[0, 1] * b + probe[1, 0] * c + probe[1, 1] * d, shift, 1)
-        tbuf[p, 1, T:T + N] = pltpu.roll(probe[0, 0] * b - probe[0, 1] * a + probe[1, 0] * d - probe[1, 1] * c, shift, 1)
+        place(p, 0, probe[0, 0] * a + probe[0, 1] * b + probe[1, 0] * c + probe[1, 1] * d)
+        place(p, 1, probe[0, 0] * b - probe[0, 1] * a + probe[1, 0] * d - probe[1, 1] * c)
 
     def scatter(s):
-        def step(n, carry):
-            q, start = 2 * s + n // (EXT // B), lax.rem(n, EXT // B) * B
-            sums = [jnp.zeros((B // 8, 8, N), F32) for _ in range(CH)]
-            for p in range(RMAX):
-                t = tbuf[p, q, pl.ds(T - plan[p, 3] + start, B), :].reshape(B // 8, 8, N)
-                for k in range(CH):
-                    sums[k] = sums[k] + t * masks[p, k]
-            for k in range(CH):
-                acc[q, k, pl.ds(pl.multiple_of(start, B), B), :] = sums[k].reshape(B, N)
-            return carry
-
-        lax.fori_loop(0, 2 * (EXT // B), step, 0)
+        for n in range(2 * THIRDS // 2):
+            acc[s, :, n * T:(n + 1) * T] = dot(rows[...], parts[:, n * T:(n + 1) * T])
+
+    def sums(s, q, k, start, size):
+        n = THIRDS * q + k % THIRDS
+        return acc[s, start:start + size, n * N:(n + 1) * N]
 
     def send_border(s):
         for n, (dr, dc) in enumerate(SIDES):
@@ -303,10 +345,10 @@
             if dc == 0:
                 for q in range(2):
                     for j in range(2):
-                        f0[n, s, q, j] = acc[2 * s + q, 1 + j, start:start + size].astype(BF16)
+                        f0[n, s, q, j] = sums(s, q, 1 + j, start, size).astype(BF16)
             else:
                 j = 0 if dc < 0 else 3
-                x = pack(acc[2 * s, j, start:start + size], acc[2 * s + 1, j, start:start + size], dc < 0)
+                x = pack(sums(s, 0, j, start, size), sums(s, 1, j, start, size), dc < 0)
                 if n < 4:
                     f1[n - 2, s] = x
                 else:
@@ -316,7 +358,7 @@
     def add_border(s, copies):
         for q in range(2):
             for j in range(2):
-                out[2 * s + q, :, j * N:(j + 1) * N] = acc[2 * s + q, 1 + j, B:B + T]
+                out[2 * s + q, :, j * N:(j + 1) * N] = sums(s, q, 1 + j, B, T)
         for n, (dr, dc) in enumerate(SIDES):
             copies[n].wait()
             there = exists((-dr, -dc))
@@ -334,12 +376,11 @@
                 out[2 * s + 1, start:start + size, j * N:(j + 1) * N] += jnp.where(mine, pltpu.roll(x, B, 1), 0.0)
 
     unpack_object(0)
-    amp_copies = [send(s_amp.at[k], got_amp.at[k], (0, offset)) for k, offset in enumerate(REACH)]
     each(first)
+    pass_on()
     unpack_object(1)
     each(second)
-    for copy in amp_copies:
-        copy.wait()
+    end_amps()
     each(third)
     scatter(1)
     late = send_border(1)
@@ -367,12 +408,12 @@
             vmem((4, T, T), F32), vmem((COUNT, N, N), BF16), *[smem((1, 1, COUNT), i32)] * 3,
             vmem((2, 2, N, N), F32), vmem((4, 2 * N, 2 * N), BF16), vmem((4, T, T), F32),
             vmem((4, CH, EXT, N), F32), *side_buffers(), *side_buffers(), *side_buffers(), *side_buffers(),
-            vmem((KINDS, CAP, N, N), BF16), vmem((KINDS, CAP, N, N), BF16),
+            vmem((KINDS, CAP, N, N), BF16), vmem((KINDS, CAP, N, N), BF16), vmem((CAP, N, N), BF16),
             vmem((KINDS, 8, N), i32), vmem((KINDS, 8, N), i32), smem((KINDS, 8, N), i32), smem((RMAX, 8), i32),
-            vmem((RMAX, CH, 8, N), F32), vmem((RMAX, 2 * N, 2 * N), F32), vmem((RMAX, 2 * N, 2 * N), F32),
+            vmem((RMAX, THIRDS, 8, N), F32), vmem((RMAX, 2 * N, 2 * N), F32), vmem((RMAX, 2 * N, 2 * N), F32),
             vmem((RMAX, 2, N, N), F32), vmem((RMAX, 2 * N, 2 * N), BF16),
-            vmem((RMAX, 4, 2 * T + N, N), F32), vmem((4, CH, EXT, N), F32),
-            pltpu.SemaphoreType.DMA((2, 2 * KINDS + 4 * len(SIDES))), pltpu.SemaphoreType.DMA((11,)),
+            vmem((EXT, RMAX * N), BF16), vmem((RMAX * N, 2 * THIRDS * N), BF16), vmem((2, EXT, 2 * THIRDS * N), F32),
+            pltpu.SemaphoreType.DMA((2, 4 * KINDS + 4 * len(SIDES))), pltpu.SemaphoreType.DMA((11,)),
         ],
         compiler_params=pltpu.CompilerParams(collective_id=0, has_side_effects=True, vmem_limit_bytes=56 << 20),
     )(objects.reshape(4, T, T), amplitudes.reshape(COUNT, N, N), owners, off_rows, off_cols, probe, tables())

time: 67.6 us -> 62.1 us (0.919)
  Pallas kernels: 64.5 us -> 58.7 us
    pallas_call x1, Pallas kernels: 64.5 us -> 58.7 us  [local(): pl.pallas_call(kernel, out_shape=jax.ShapeDtypeStruct((4, T, T), F32), in...]
where the time goes in v3:
time: 62.1 us; the launch traced here: 61 us
  Pallas kernels  58.7 us (95%)
  local copies, waits for them, and re-layouts  2.29 us (4%)
    pallas_call x1, Pallas kernels, local(): pl.pallas_call(kernel, out_shape=jax.ShapeDtypeStruct((4, T, T), F32), in...  58.7 us
    unnamed x1, local copies, waits for them, and re-layouts  2.29 us

profile of v3, /device:TPU:1, one launch (start us, length us, event | category | flops | bytes accessed | tf_op | source)
XLA Modules:
  0.0 61.0 jit_solution(10390176699255730370)
XLA Ops:
  0.0 58.7 %shard_map.73 = f32[4,256,256]{2,1,0:T(8,128)} custom-call(f32[4,256,256]{2,1,0:T(8,128)} %bitcast.4, bf16[6,128,128]{2,1,0:T(8,128)(2,1)} %bitcast.5, s32[1,1,6]{2,1,0:T(1,128)} %own_h.1, s32[1,1,6]{2,1,0:T(1,128)} %offr_h.1, s32[1,1,6]{2,1,0:T(1,128)} %offc_h.1, f32[2,2,128,128]{3,2,1,0:T(8,128)} %probe_h.1, bf16[4,256,256]{2,1,0:T(8,128)(2,1)} %constant.7.mats_h), custom_call_target="tpu_custom_call" | custom-call | tf_op jit(solution)/shard_map/pallas_call | solution.py:402
  58.7 2.3 %copy.9 = f32[2,2,256,256]{3,2,1,0:T(8,128)} copy(f32[2,2,256,256]{3,2,1,0:T(8,128)} %bitcast.3) | data formatting | bytes 2097152

commit v4 on v3

--- a/solution.py
+++ b/solution.py
@@ -27,7 +27,7 @@
 XS = 8
 PARTNERS = SIDES + tuple((0, d) for d in (-4, -3, -2, 2, 3, 4, -XS, XS))
 THIRDS = 3
-GROUP = 6
+GROUP = 12
 
 
 def tables():
@@ -375,9 +375,9 @@
                 out[2 * s, start:start + size, j * N:(j + 1) * N] += jnp.where(mine, x, 0.0)
                 out[2 * s + 1, start:start + size, j * N:(j + 1) * N] += jnp.where(mine, pltpu.roll(x, B, 1), 0.0)
 
+    pass_on()
     unpack_object(0)
     each(first)
-    pass_on()
     unpack_object(1)
     each(second)
     end_amps()

time: 62.1 us -> 60.7 us (0.977)
  the two profiles are of different devices: /device:TPU:1 before, /device:TPU:49 now
where the time goes in v4:
time: 60.7 us; the launch traced here: 60.6 us
  Pallas kernels  58.3 us (96%)
  local copies, waits for them, and re-layouts  2.29 us (4%)
    pallas_call x1, Pallas kernels, local(): pl.pallas_call(kernel, out_shape=jax.ShapeDtypeStruct((4, T, T), F32), in...  58.3 us
    unnamed x1, local copies, waits for them, and re-layouts  2.29 us

profile of v4, /device:TPU:49, one launch (start us, length us, event | category | flops | bytes accessed | tf_op | source)
XLA Modules:
  0.0 60.6 jit_solution(6235487512167222703)
XLA Ops:
  0.0 58.3 %shard_map.73 = f32[4,256,256]{2,1,0:T(8,128)} custom-call(f32[4,256,256]{2,1,0:T(8,128)} %bitcast.4, bf16[6,128,128]{2,1,0:T(8,128)(2,1)} %bitcast.5, s32[1,1,6]{2,1,0:T(1,128)} %own_h.1, s32[1,1,6]{2,1,0:T(1,128)} %offr_h.1, s32[1,1,6]{2,1,0:T(1,128)} %offc_h.1, f32[2,2,128,128]{3,2,1,0:T(8,128)} %probe_h.1, bf16[4,256,256]{2,1,0:T(8,128)(2,1)} %constant.7.mats_h), custom_call_target="tpu_custom_call" | custom-call | tf_op jit(solution)/shard_map/pallas_call | solution.py:402
  58.3 2.3 %copy.9 = f32[2,2,256,256]{3,2,1,0:T(8,128)} copy(f32[2,2,256,256]{3,2,1,0:T(8,128)} %bitcast.3) | data formatting | bytes 2097152

commit v5 on v4

--- a/solution.py
+++ b/solution.py
@@ -149,10 +149,6 @@
     pack_object(0)
     pl.semaphore_wait(barrier, len(PARTNERS))
     halo = [[send(buffer_of((s0, s1, s2), n, 0), buffer_of((r0, r1, r2), n, 0), side) for n, side in enumerate(SIDES)]]
-    in_obj[1].wait()
-    pack_object(1)
-    halo.append([send(buffer_of((s0, s1, s2), n, 1), buffer_of((r0, r1, r2), n, 1), side) for n, side in enumerate(SIDES)])
-
     for copy in in_ints:
         copy.wait()
     dest = [own[0, 0, j] for j in range(COUNT)]
@@ -227,6 +223,9 @@
                 straight[k].wait_send()
 
     start_amps()
+    in_obj[1].wait()
+    pack_object(1)
+    halo.append([send(buffer_of((s0, s1, s2), n, 1), buffer_of((r0, r1, r2), n, 1), side) for n, side in enumerate(SIDES)])
 
     for q in range(4):
         for j in range(2):

time: 60.7 us -> 61.1 us (level)
  the two profiles are of different devices: /device:TPU:49 before, /device:TPU:1 now
where the time goes in v5:
time: 61.1 us; the launch traced here: 60.9 us
  Pallas kernels  58.7 us (96%)
  local copies, waits for them, and re-layouts  2.29 us (4%)
    pallas_call x1, Pallas kernels, local(): pl.pallas_call(kernel, out_shape=jax.ShapeDtypeStruct((4, T, T), F32), in...  58.7 us
    unnamed x1, local copies, waits for them, and re-layouts  2.29 us

profile of v5, /device:TPU:1, one launch (start us, length us, event | category | flops | bytes accessed | tf_op | source)
XLA Modules:
  0.0 60.9 jit_solution(301494774700142676)
XLA Ops:
  0.0 58.7 %shard_map.73 = f32[4,256,256]{2,1,0:T(8,128)} custom-call(f32[4,256,256]{2,1,0:T(8,128)} %bitcast.4, bf16[6,128,128]{2,1,0:T(8,128)(2,1)} %bitcast.5, s32[1,1,6]{2,1,0:T(1,128)} %own_h.1, s32[1,1,6]{2,1,0:T(1,128)} %offr_h.1, s32[1,1,6]{2,1,0:T(1,128)} %offc_h.1, f32[2,2,128,128]{3,2,1,0:T(8,128)} %probe_h.1, bf16[4,256,256]{2,1,0:T(8,128)(2,1)} %constant.7.mats_h), custom_call_target="tpu_custom_call" | custom-call | tf_op jit(solution)/shard_map/pallas_call | solution.py:401
  58.7 2.3 %copy.9 = f32[2,2,256,256]{3,2,1,0:T(8,128)} copy(f32[2,2,256,256]{3,2,1,0:T(8,128)} %bitcast.3) | data formatting | bytes 2097152
